TPU v7x, 128 devices: a whole 4x4x4 slice. The times are simulated.
128 devices in a mesh: space: 32 (over y, x, core), tx: 4 (over z).
Axes of the slice: x: 4, y: 4, z: 4, core: 2. Of those that a mesh axis runs over, the one named last changes fastest.
Arguments:
- conductivity: float32 [64, 128, 256], P('space'), may hold values from 0.25 to 2
- chargeability: float32 [64, 128, 256], P('space'), may hold values from 0.05 to 0.6
- relaxation: float32 [64, 128, 256], P('space'), may hold values from 0.5 to 8
- start_potential: float32 [8, 64, 128, 256], P('tx', 'space'), may hold values from 0 to 2
- start_memory: float32 [4, 8, 64, 128, 256], P(None, 'tx', 'space'), may hold values from -6 to 6
- source_cells: int32 [2, 8], P(None, 'tx'), may hold values from 0 to 2097151
- dipole_cells: int32 [2, 4096], replicated, may hold values from 0 to 2097151
- live_counts: int32 [32], replicated, may hold values from 32 to 128, as said below
- observed: float32 [3, 8, 4096], P(None, 'tx', 'space'), may hold values from -4 to 4
Outputs:
- voltages: float32 [3, 8, 4096], P(None, 'tx', 'space')
- misfit: float32 [], replicated
- grad_chargeability: float32 [64, 128, 256], P('space', 'tx')
- grad_relaxation: float32 [64, 128, 256], P('space', 'tx')
Inputs may be any that keep to these rules, and one draw needn't show every extreme that they name: `source_cells`: flat cell indices of the grid. `dipole_cells`: flat cell indices of the grid. `live_counts`: some slab has all 128 slots live.
All inputs are finite; a program needn't handle non-finite values.
Results may differ from a plain program's by a relative error of at most 0.00002.
Values sent between devices are 32-bit elements; how exact they have to be, the bound alone decides.
A program may use at most 192 MiB of HBM per device.

v0:
```python
import jax
import jax.numpy as jnp
from jax import lax
from jax.sharding import PartitionSpec as P

NSTEPS = 3
JACOBI = 8


mode_weights = (0.4, 0.3, 0.2, 0.1)
mode_ratios = (0.25, 1.0, 4.0, 16.0)
strength = 4.0


def extended(array, sides, width):
    for axis, dim in sides:
        peers, length = (lax.axis_size(axis), array.shape[dim])
        up = [(i, (i + 1) % peers) for i in range(peers - 1)]
        down = [(j, i) for i, j in up]
        last = lax.slice_in_dim(array, length - width, length, axis=dim)
        initial = lax.slice_in_dim(array, 0, width, axis=dim)
        before = lax.ppermute(last, axis, up)
        after = lax.ppermute(initial, axis, down)
        array = jnp.concatenate([before, array, after], axis=dim)
    return array


def neighbours(padded):
    core = padded[:, 1:-1]
    total = padded[:, 2:] + padded[:, :-2]
    side_y = jnp.pad(core, ((0, 0), (0, 0), (1, 1), (0, 0)))
    total = total + side_y[:, :, 2:] + side_y[:, :, :-2]
    side_z = jnp.pad(core, ((0, 0), (0, 0), (0, 0), (1, 1)))
    return total + side_z[..., 2:] + side_z[..., :-2]


def rim_one(field):
    return extended(field, (("space", 1),), 1)


def total_misfit(partial_value):
    return jnp.sqrt(1.0 + lax.psum(partial_value, ("space", "tx")))


def on_device(
    conductivity,
    chargeability,
    relaxation,
    start_potential,
    start_memory,
    source_cells,
    dipole_cells,
    live_counts,
    observed,
):
    slots = start_potential.shape[0]
    cells = conductivity.size
    tile = lax.axis_index("space")
    first = tile * cells
    inverse = 1.0 / (6.0 + conductivity)

    def local_index(global_cells):
        shifted = global_cells - first
        inside = ((shifted >= 0) & (shifted < cells)).astype(jnp.float32)
        return (jnp.clip(shifted, 0, cells - 1), inside)

    slot_ids = jnp.arange(slots, dtype=jnp.int32)
    place_a, inside_a = local_index(source_cells[0])
    place_b, inside_b = local_index(source_cells[1])
    source = jnp.zeros((slots, cells), jnp.float32).at[slot_ids, place_a].add(strength * inside_a)
    source = source.at[slot_ids, place_b].add(-strength * inside_b).reshape(start_potential.shape)
    probe_one, inside_one = local_index(dipole_cells[0])
    probe_two, inside_two = local_index(dipole_cells[1])
    decays = [jnp.exp(-1.0 / (relaxation * ratio)) for ratio in mode_ratios]
    couple = [chargeability * mode_weights[level] * (1.0 - decays[level]) for level in range(4)]
    slopes = [decays[level] / (mode_ratios[level] * relaxation * relaxation) for level in range(4)]
    memory = [start_memory[level] for level in range(4)]
    potential = start_potential
    kept_potential = []
    kept_memory = []
    partials = []
    for step in range(NSTEPS):
        stored = memory[0] + memory[1] + memory[2] + memory[3]
        if step == 0:
            rhs = source + conductivity * stored
        else:
            rhs = conductivity * stored
        forward_field = potential
        for forward_sweep in range(JACOBI):
            forward_field = (rhs + neighbours(rim_one(forward_field))) * inverse
        potential = forward_field
        kept_potential.append(potential)
        kept_memory.append(memory)
        memory = [decays[level] * memory[level] + couple[level] * potential for level in range(4)]
        flat = potential.reshape(slots, cells)
        partials.append(
            jnp.take(flat, probe_one, axis=1) * inside_one
            - jnp.take(flat, probe_two, axis=1) * inside_two
        )
    volts = lax.psum_scatter(jnp.stack(partials), "space", scatter_dimension=2, tiled=True)
    receivers = observed.shape[2]
    live = (jnp.arange(receivers) < live_counts[tile]).astype(jnp.float32)
    volts = volts * live
    resid = live * (volts - observed)
    partial_value = jnp.sum(resid * resid)
    misfit = total_misfit(partial_value)
    pulled = resid / misfit
    spread = lax.all_gather(pulled, "space", axis=2, tiled=True)
    back = jnp.zeros_like(start_potential)
    duals = [jnp.zeros_like(start_potential) for level in range(4)]
    grad_c = jnp.zeros_like(start_potential)
    grad_t = jnp.zeros_like(start_potential)
    for step in reversed(range(NSTEPS)):
        current = kept_potential[step]
        before = kept_memory[step]
        inject = jnp.zeros((slots, cells), jnp.float32)
        inject = inject.at[:, probe_one].add(spread[step] * inside_one)
        inject = (
            inject.at[:, probe_two].add(-spread[step] * inside_two).reshape(start_potential.shape)
        )
        incoming = back + inject
        for level in range(4):
            incoming = incoming + couple[level] * duals[level]
            grad_c = grad_c + duals[level] * mode_weights[level] * (1.0 - decays[level]) * current
            grad_t = grad_t + duals[level] * slopes[level] * (
                before[level] - chargeability * mode_weights[level] * current
            )
        duals = [decays[level] * duals[level] for level in range(4)]
        field = incoming
        summed = jnp.zeros_like(incoming)
        for sweep in range(JACOBI):
            scaled = field * inverse
            summed = summed + scaled
            field = neighbours(rim_one(scaled))
        summed, back = (summed, field)
        duals = [duals[level] + conductivity * summed for level in range(4)]
    grad_charge, grad_relax = (
        lax.psum_scatter(jnp.sum(grad_c, axis=0), "tx", scatter_dimension=1, tiled=True),
        lax.psum_scatter(jnp.sum(grad_t, axis=0), "tx", scatter_dimension=1, tiled=True),
    )
    return (volts, misfit, grad_charge, grad_relax)


def solution(mesh):
    placed = (
        P("space", None, None),
        P("space", None, None),
        P("space", None, None),
        P("tx", "space", None, None),
        P(None, "tx", "space", None, None),
        P(None, "tx"),
        P(),
        P(),
        P(None, "tx", "space"),
    )
    return jax.shard_map(
        on_device,
        mesh=mesh,
        in_specs=placed,
        out_specs=(P(None, "tx", "space"), P(), P("space", "tx", None), P("space", "tx", None)),
        check_vma=False,
    )
```

profile of v0, /device:TPU:19, one launch (start us, length us, event | category | flops | bytes accessed | tf_op | source)
XLA Modules:
  0.0 1154.0 jit_solution(7150294656307960920)
XLA Ops:
  43.2 6.5 collective-permute-start.6
  55.3 6.5 collective-permute-start.8
  67.5 6.5 collective-permute-start.10
  79.6 6.5 collective-permute-start.12
  91.8 6.6 collective-permute-start.14
  104.1 6.5 collective-permute-start.16
  116.6 6.5 collective-permute-start.18
  128.7 6.5 collective-permute-start.20
  140.9 6.5 collective-permute-start.22
  153.0 6.5 collective-permute-start.24
  165.2 6.5 collective-permute-start.26
  177.3 6.5 collective-permute-start.28
  189.5 6.6 collective-permute-start.30
  201.8 6.5 collective-permute-start.32
  214.5 6.5 collective-permute-start.34
  226.6 6.5 collective-permute-start.36
  238.8 6.5 collective-permute-start.38
  250.9 6.5 collective-permute-start.40
  263.1 6.5 collective-permute-start.42
  275.2 6.5 collective-permute-start.44
  297.4 16.6 %copy.44 = f32[2,2,128,256]{0,3,2,1:T(8,128)} copy(f32[2,2,128,256]{3,2,1,0:T(8,128)S(1)} %fusion.73) | data formatting | bytes 1048576 | tf_op jit(solution)/shard_map/mul | solution.py:90
  314.0 24.7 %gather_fusion.1 = f32[4096,2]{1,0:T(8,128)} fusion(f32[2,65536]{0,1:T(8,128)} %bitcast.195, s32[4096]{0:T(1024)S(1)} %fusion.321), kind=kCustom, calls=%fused_computation.1.clone | custom fusion | bytes 81920 | tf_op jit(solution)/shard_map/jit(_take)/gather | solution.py:98
  338.7 24.7 %gather_fusion = f32[4096,2]{1,0:T(8,128)} fusion(f32[2,65536]{0,1:T(8,128)} %bitcast.196, s32[4096]{0:T(1024)S(1)} %fusion.320), kind=kCustom, calls=%fused_computation.clone | custom fusion | bytes 81920 | tf_op jit(solution)/shard_map/jit(_take)/gather | solution.py:97
  363.4 17.4 %copy.45 = f32[2,2,128,256]{0,3,2,1:T(8,128)} copy(f32[2,2,128,256]{3,2,1,0:T(8,128)} %copy-done.1) | data formatting | bytes 1048576 | tf_op jit(solution)/shard_map/mul | solution.py:90
  380.8 24.7 %gather_fusion.3 = f32[4096,2]{1,0:T(8,128)} fusion(f32[2,65536]{0,1:T(8,128)} %bitcast.197, s32[4096]{0:T(1024)S(1)} %fusion.321), kind=kCustom, calls=%fused_computation.3.clone | custom fusion | bytes 81920 | tf_op jit(solution)/shard_map/jit(_take)/gather | solution.py:98
  405.6 24.7 %gather_fusion.2 = f32[4096,2]{1,0:T(8,128)} fusion(f32[2,65536]{0,1:T(8,128)} %bitcast.198, s32[4096]{0:T(1024)S(1)} %fusion.320), kind=kCustom, calls=%fused_computation.2.clone | custom fusion | bytes 81920 | tf_op jit(solution)/shard_map/jit(_take)/gather | solution.py:97
  433.9 17.4 %copy.46 = f32[2,2,128,256]{0,3,2,1:T(8,128)} copy(f32[2,2,128,256]{3,2,1,0:T(8,128)} %fusion.169) | data formatting | bytes 1048576 | tf_op jit(solution)/shard_map/mul | solution.py:90
  451.3 24.7 %gather_fusion.5 = f32[4096,2]{1,0:T(8,128)} fusion(f32[2,65536]{0,1:T(8,128)} %bitcast.193, s32[4096]{0:T(1024)S(1)} %fusion.321), kind=kCustom, calls=%fused_computation.5.clone | custom fusion | bytes 81920 | tf_op jit(solution)/shard_map/jit(_take)/gather | solution.py:98
  476.1 24.7 %gather_fusion.4 = f32[4096,2]{1,0:T(8,128)} fusion(f32[2,65536]{0,1:T(8,128)} %bitcast.194, s32[4096]{0:T(1024)S(1)} %fusion.320), kind=kCustom, calls=%fused_computation.4.clone | custom fusion | bytes 81920 | tf_op jit(solution)/shard_map/jit(_take)/gather | solution.py:97
  511.7 86.8 %reduce-scatter.4.cloned.1.call-done = f32[3,2,128]{1,2,0:T(8,128)} async-done(((f32[3,2,4096]{1,2,0:T(8,128)}), f32[3,2,128]{1,2,0:T(8,128)}) %reduce-scatter.4.cloned.1.call-update) | async-done | bytes 3088 | tf_op jit(solution)/shard_map/reduce_scatter | solution.py:100
  600.2 64.8 %psum.7 = f32[]{:T(128)} all-reduce(f32[]{:T(128)} %multiply_reduce_fusion), channel_id=1, replica_groups=mesh['space'=32,'tx'=4] {'space','tx'}, use_global_device_ids=true, to_apply=%region_4.6 | all-reduce | flops 1 | bytes 8 | tf_op jit(solution)/shard_map/psum | solution.py:42
  667.3 32.4 %all_gather.3 = f32[3,2,4096]{1,2,0:T(8,128)} all-gather(f32[3,2,128]{1,2,0:T(8,128)S(1)} %get-tuple-element.175), channel_id=1, replica_groups=mesh['space'=32,'tx'=4] {'space'}, dimensions={2}, use_global_device_ids=true | all-gather | bytes 101376 | tf_op jit(solution)/shard_map/all_gather | solution.py:108
  699.7 38.0 %scatter_custom_fusion.2 = f32[2,65536]{0,1:T(8,128)} fusion(s32[4096]{0:T(1024)S(1)} %bitcast.213, f32[]{:T(128)} %constant.26.clone.1, f32[3,2,4096]{1,2,0:T(8,128)} %all_gather.3, f32[4096]{0:T(1024)S(1)} %bitcast.205), kind=kCustom, calls=%fused_computation.14 | custom fusion | flops 16384 | bytes 2638336 | tf_op jit(solution)/shard_map/scatter-add | solution.py:117
  737.7 45.1 %scatter_custom_fusion.3 = f32[2,65536]{0,1:T(8,128)} fusion(f32[2,65536]{0,1:T(8,128)} %scatter_custom_fusion.2, s32[4096]{0:T(1024)S(1)} %bitcast.211, f32[3,2,4096]{1,2,0:T(8,128)} %all_gather.3, f32[4096]{0:T(1024)S(1)} %bitcast.202), kind=kCustom, calls=%fused_computation.22 | custom fusion | flops 24576 | bytes 2637824 | tf_op jit(solution)/shard_map/scatter-add | solution.py:119
  782.7 19.4 %copy.49 = f32[2,2,128,256]{3,2,1,0:T(8,128)S(1)} copy(f32[2,2,128,256]{0,3,2,1:T(8,128)} %bitcast.192) | data formatting | bytes 1048576 | tf_op jit(solution)/shard_map/reshape | solution.py:119
  823.0 6.6 collective-permute-start.52
  835.3 6.5 collective-permute-start.54
  847.4 6.5 collective-permute-start.56
  859.5 6.5 collective-permute-start.58
  893.2 38.1 %scatter_custom_fusion.4 = f32[2,65536]{0,1:T(8,128)} fusion(s32[4096]{0:T(1024)S(1)} %bitcast.214, f32[]{:T(128)} %constant.26.clone.1, f32[3,2,4096]{1,2,0:T(8,128)} %all_gather.3, f32[4096]{0:T(1024)S(1)} %bitcast.206), kind=kCustom, calls=%fused_computation.12 | custom fusion | flops 16384 | bytes 2638336 | tf_op jit(solution)/shard_map/scatter-add | solution.py:117
  931.3 45.1 %scatter_custom_fusion.5 = f32[2,65536]{0,1:T(8,128)} fusion(f32[2,65536]{0,1:T(8,128)} %scatter_custom_fusion.4, s32[4096]{0:T(1024)S(1)} %bitcast.212, f32[3,2,4096]{1,2,0:T(8,128)} %all_gather.3, f32[4096]{0:T(1024)S(1)} %bitcast.203), kind=kCustom, calls=%fused_computation.19 | custom fusion | flops 24576 | bytes 2637824 | tf_op jit(solution)/shard_map/scatter-add | solution.py:119
  976.4 20.2 %copy.51 = f32[2,2,128,256]{3,2,1,0:T(8,128)} copy(f32[2,2,128,256]{0,3,2,1:T(8,128)} %bitcast.191) | data formatting | bytes 1048576 | tf_op jit(solution)/shard_map/reshape | solution.py:119
  996.6 8.1 fusion.214
  1025.8 8.6 collective-permute-start.68
  1052.2 6.6 collective-permute-start.72
  1064.6 6.8 collective-permute-start.74
  1099.3 23.3 %reduce-scatter.8.cloned.1.call-done = f32[2,32,256]{2,1,0:T(8,128)} async-done(((f32[2,128,256]{2,1,0:T(8,128)}), f32[2,32,256]{2,1,0:T(8,128)}) %reduce-scatter.8.cloned.1.call-update) | async-done | bytes 65552 | tf_op jit(solution)/shard_map/reduce_scatter | solution.py:139
  1122.7 23.4 %reduce-scatter.6.cloned.1.call-done = f32[2,32,256]{2,1,0:T(8,128)} async-done(((f32[2,128,256]{2,1,0:T(8,128)}), f32[2,32,256]{2,1,0:T(8,128)}) %reduce-scatter.6.cloned.1.call-update) | async-done | bytes 65552 | tf_op jit(solution)/shard_map/reduce_scatter | solution.py:138
  (355 shorter events, 313.3 us)
Async XLA Ops:
  7.2 591.3 %reduce-scatter.4.cloned.1.call-start = ((), (), s32[]{:S(2)}) async-start(), calls=%async_computation.3 | async-start | bytes 6488064 | tf_op jit(solution)/shard_map/reduce_scatter | solution.py:100
  9.1 8.8 collective-permute-start
  11.8 6.6 collective-permute-start.1
  21.1 8.4 collective-permute-start.2
  24.4 6.3 collective-permute-start.3
  31.2 8.4 collective-permute-start.4
  43.2 8.4 collective-permute-start.6
  55.3 8.4 collective-permute-start.8
  67.5 8.4 collective-permute-start.10
  79.6 8.4 collective-permute-start.12
  91.8 8.6 collective-permute-start.14
  104.1 11.4 collective-permute-start.16
  116.6 8.4 collective-permute-start.18
  128.7 8.4 collective-permute-start.20
  140.9 8.4 collective-permute-start.22
  153.0 8.4 collective-permute-start.24
  165.2 8.4 collective-permute-start.26
  177.3 8.4 collective-permute-start.28
  189.5 8.6 collective-permute-start.30
  201.8 8.6 collective-permute-start.32
  214.5 8.4 collective-permute-start.34
  226.6 8.4 collective-permute-start.36
  238.8 8.4 collective-permute-start.38
  250.9 8.4 collective-permute-start.40
  263.1 8.5 collective-permute-start.42
  275.2 8.5 collective-permute-start.44
  288.9 141.3 %collective-permute-start.46 = (f32[2,1,128,256]{3,2,1,0:T(8,128)}, f32[2,1,128,256]{3,2,1,0:T(8,128)}, u32[]{:S(2)}, u32[]{:S(2)}) collective-permute-start(f32[2,1,128,256]{3,2,1,0:T(8,128)} %get-tuple-element.81), channel_id=1, source_target_pairs={{4,0},{8,4},{12,8},{16,12},{20,16},{24,20},{28,24},{32,28},{36,32}... | collective-permute-start | bytes 786440 | tf_op jit(solution)/shard_map/ppermute | solution.py:23
  295.4 134.8 %collective-permute-start.47 = (f32[2,1,128,256]{3,2,1,0:T(8,128)}, f32[2,1,128,256]{3,2,1,0:T(8,128)}, u32[]{:S(2)}, u32[]{:S(2)}) collective-permute-start(f32[2,1,128,256]{3,2,1,0:T(8,128)} %get-tuple-element.82), channel_id=1, source_target_pairs={{0,4},{4,8},{8,12},{12,16},{16,20},{20,24},{24,28},{28,32},{32,36}... | collective-permute-start | bytes 786440 | tf_op jit(solution)/shard_map/ppermute | solution.py:22
  509.7 613.0 %reduce-scatter.8.cloned.1.call-start = ((), (), s32[]{:S(2)}) async-start(), calls=%async_computation.5 | async-start | bytes 327680 | tf_op jit(solution)/shard_map/reduce_scatter | solution.py:139
  803.7 8.0 collective-permute-start.48
  805.7 6.9 collective-permute-start.49
  813.0 8.4 collective-permute-start.50
  823.0 8.5 collective-permute-start.52
  835.3 8.4 collective-permute-start.54
  847.4 8.4 collective-permute-start.56
  859.5 8.4 collective-permute-start.58
  871.7 8.4 collective-permute-start.60
  884.7 111.8 %collective-permute-start.62 = (f32[2,1,128,256]{3,2,1,0:T(8,128)}, f32[2,1,128,256]{3,2,1,0:T(8,128)}, u32[]{:S(2)}, u32[]{:S(2)}) collective-permute-start(f32[2,1,128,256]{3,2,1,0:T(8,128)} %get-tuple-element.65), channel_id=1, source_target_pairs={{4,0},{8,4},{12,8},{16,12},{20,16},{24,20},{28,24},{32,28},{36,32}... | collective-permute-start | bytes 786440 | tf_op jit(solution)/shard_map/ppermute | solution.py:23
  891.2 105.3 %collective-permute-start.63 = (f32[2,1,128,256]{3,2,1,0:T(8,128)}, f32[2,1,128,256]{3,2,1,0:T(8,128)}, u32[]{:S(2)}, u32[]{:S(2)}) collective-permute-start(f32[2,1,128,256]{3,2,1,0:T(8,128)} %get-tuple-element.66), channel_id=1, source_target_pairs={{0,4},{4,8},{8,12},{12,16},{16,20},{20,24},{24,28},{28,32},{32,36}... | collective-permute-start | bytes 786440 | tf_op jit(solution)/shard_map/ppermute | solution.py:22
  1004.7 7.7 collective-permute-start.64
  1007.0 6.6 collective-permute-start.65
  1014.0 8.4 collective-permute-start.66
  1025.8 10.5 collective-permute-start.68
  1040.0 8.4 collective-permute-start.70
  1052.2 8.6 collective-permute-start.72
  1064.6 8.7 collective-permute-start.74
  1077.0 8.4 collective-permute-start.76
  1094.7 51.5 %reduce-scatter.6.cloned.1.call-start = ((), (), s32[]{:S(2)}) async-start(), calls=%async_computation.4 | async-start | bytes 327680 | tf_op jit(solution)/shard_map/reduce_scatter | solution.py:138
  (93 other events, 2088.7 us)
Sparse Core Ops, SparseCore 0:
  509.8 88.6 reduce-scatter.3
  1094.8 27.8 reduce-scatter.7
  1125.6 20.4 reduce-scatter.5
where the time goes:
time: 1170 us; the launch traced here: 1150 us
  starting transfers between devices  319 us (27%)
  waiting for transfers between devices  249 us (21%)
  local copies, waits for them, and re-layouts  248 us (21%)
  other arithmetic  224 us (19%)
  blocking collectives  97.2 us (8%)
  between operations  18 us (2%)
    ppermute x39, starting transfers between devices, extended(): after = lax.ppermute(initial, axis, down)  238 us
    ppermute x39, waiting for transfers between devices, extended(): before = lax.ppermute(last, axis, up)  106 us
    scatter-add x2, other arithmetic, on_device(): inject.at[:, probe_two].add(-spread[step] * inside_two)  90.1 us
    reduce_scatter x1, waiting for transfers between devices, on_device(): lax.psum_scatter(jnp.stack(partials), 'space', scatter_dimension=2, tiled...  86.8 us
    ppermute x39, starting transfers between devices, extended(): before = lax.ppermute(last, axis, up)  81.1 us
    scatter-add x2, other arithmetic, on_device(): inject = inject.at[:, probe_one].add(spread[step] * inside_one)  76.1 us
    gather x3, local copies, waits for them, and re-layouts, on_device(): jnp.take(flat, probe_one, axis=1) * inside_one  74.2 us
    gather x3, local copies, waits for them, and re-layouts, on_device(): jnp.take(flat, probe_two, axis=1) * inside_two  74.1 us
  transfers between devices with their start and end apart: 81, of which 46 were waited for; matrix products, arithmetic and copies ran while one was open for 22% of the time, Pallas kernels for 0%

commit v1 on v0

v1 whole, which is shorter than its diff:
```python
import functools

import jax
import jax.numpy as jnp
from jax import lax
from jax.experimental import pallas as pl
from jax.experimental.pallas import tpu as pltpu
from jax.sharding import PartitionSpec as P

MESH = pl.DeviceIdType.MESH
F32 = jnp.float32
BF16 = jnp.bfloat16
NSTEPS = 3
JACOBI = 8
WEIGHTS = (0.4, 0.3, 0.2, 0.1)
RATIOS = (0.25, 1.0, 4.0, 16.0)
STRENGTH = 4.0

GY, GX = 4, 4
SLOTS = 2 * GX
BX, BY, LANES = 16, 32, 128
TOP = 8
NDIP = 4096
CHUNK = 512
ROWS = BX * BY
U0, R0, R1, R2, T1, T2 = range(6)
COND, CHG, RLX = range(3)


def remote(src, dst, send, recv, device):
    return pltpu.make_async_remote_copy(
        src_ref=src, dst_ref=dst, send_sem=send, recv_sem=recv, device_id=device, device_id_type=MESH
    )


def kernel(
    cond, chg, rlx, start, mem, src_cells, dip, counts, obs,
    volts_out, misfit_out, gc_out, gt_out,
    stage, sstage, blk, sblk, v, ysend, yrecv,
    inv, rhs, f1, f2, ka0, ka1, kb0, kb1, un, adj, back,
    ut, acc, part, prx, pry, res, obs_all, live, vswap, sq, sqc, sqz,
    grad, rc, red, rx, rz,
    fsend, frecv, ssend, srecv, hsend, hrecv, osend, orecv, psend, precv, qsend, qrecv, gsend, grecv,
):
    space = lax.axis_index("space")
    tx = lax.axis_index("tx")
    gy = space // SLOTS
    slot = lax.rem(space, SLOTS)
    gx = slot // 2
    core = lax.rem(slot, 2)
    base = gy * SLOTS
    partner = base + gx * 2 + 1 - core

    def peer_slot(p):
        return lax.rem(slot + p, SLOTS)

    def pieces(body):
        def at(i, carry):
            row, layer = i // 2, lax.rem(i, 2)
            for half in range(2):
                body(row, layer, half, (layer, pl.ds(pl.multiple_of(row * BY, BY), BY), pl.ds(half * LANES, LANES)))
            return carry

        lax.fori_loop(0, 2 * GX, at, 0)

    def first_fields(row, layer, half, where):
        c = cond[where]
        sstage[COND, row, half, layer] = c
        ids = (2 * space + layer) * (128 * 256) + row * (BY * 256) + half * LANES
        ids = ids + lax.broadcasted_iota(jnp.int32, (BY, LANES), 0) * 256
        ids = ids + lax.broadcasted_iota(jnp.int32, (BY, LANES), 1)
        for t in range(2):
            stage[U0, t, row, half, layer] = start[(t,) + where]
            total = mem[(0, t) + where] + mem[(1, t) + where] + mem[(2, t) + where] + mem[(3, t) + where]
            source = jnp.where(ids == src_cells[0, t], STRENGTH, 0.0) - jnp.where(ids == src_cells[1, t], STRENGTH, 0.0)
            stage[R0, t, row, half, layer] = source + c * total

    def later_fields(row, layer, half, where):
        c = cond[where]
        relax = rlx[where]
        sstage[CHG, row, half, layer] = chg[where]
        sstage[RLX, row, half, layer] = relax
        rate = 1.0 / relax
        decays = [jnp.exp(-rate / ratio) for ratio in RATIOS]
        for t in range(2):
            first, second, slope, slope_d = (jnp.zeros((BY, LANES), F32) for _ in range(4))
            for k in range(4):
                scaled = decays[k] * mem[(k, t) + where]
                first = first + scaled
                second = second + decays[k] * scaled
                tilt = scaled * (1.0 / RATIOS[k])
                slope = slope + tilt
                slope_d = slope_d + decays[k] * tilt
            stage[R1, t, row, half, layer] = c * first
            stage[R2, t, row, half, layer] = c * second
            stage[T1, t, row, half, layer] = c * rate * rate * slope
            stage[T2, t, row, half, layer] = 2.0 * c * rate * rate * slope_d

    def field_copy(f, p):
        to = peer_slot(p)
        return remote(
            stage.at[f, lax.rem(to, 2), to // 2], blk.at[f, :, pl.ds(2 * slot, 2)],
            fsend.at[f, to], frecv.at[f, slot], {"space": base + to},
        )

    def static_copy(f, p):
        to = peer_slot(p)
        return remote(
            sstage.at[f, to // 2], sblk.at[f, :, pl.ds(2 * slot, 2)],
            ssend.at[f, to], srecv.at[f, slot], {"space": base + to},
        )

    def over_peers(body):
        def at(p, carry):
            body(p)
            return carry

        lax.fori_loop(1, SLOTS, at, 0)

    def send_field(f):
        over_peers(lambda p: field_copy(f, p).start())
        blk[f, :, pl.ds(2 * slot, 2)] = stage[f, core, gx]

    def send_static(f):
        over_peers(lambda p: static_copy(f, p).start())
        sblk[f, :, pl.ds(2 * slot, 2)] = sstage[f, gx]

    def take_field(f):
        def one(p):
            of = peer_slot(p)
            here = blk.at[f, :, pl.ds(2 * of, 2)]
            remote(here, here, fsend.at[f, of], frecv.at[f, of], {"space": base + of}).wait_recv()

        over_peers(one)

    def take_static(f):
        def one(p):
            of = peer_slot(p)
            here = sblk.at[f, :, pl.ds(2 * of, 2)]
            remote(here, here, ssend.at[f, of], srecv.at[f, of], {"space": base + of}).wait_recv()

        over_peers(one)

    pieces(first_fields)
    send_field(U0)
    send_static(COND)
    send_field(R0)
    pieces(later_fields)
    send_static(CHG)
    send_static(RLX)
    for f in (R1, R2, T1, T2):
        send_field(f)

    def obs_copy(p):
        to = peer_slot(p)
        return remote(
            vswap.at[pl.ds(3 * lax.rem(to, 2), 3)], obs_all.at[:, :, pl.ds(pl.multiple_of(space * LANES, LANES), LANES)],
            osend.at[to], orecv.at[slot], {"space": base + to},
        )

    for t in range(2):
        for n in range(NSTEPS):
            vswap[3 * t + n] = obs[n, t : t + 1, :]
    over_peers(lambda p: obs_copy(p).start())
    obs_all[:, :, pl.ds(pl.multiple_of(space * LANES, LANES), LANES)] = vswap[pl.ds(3 * core, 3)]

    def obs_wait(p):
        of = peer_slot(p)
        here = obs_all.at[:, :, pl.ds(pl.multiple_of((base + of) * LANES, LANES), LANES)]
        remote(here, here, osend.at[of], orecv.at[of], {"space": base + of}).wait_recv()

    def column_copy(p):
        to = lax.rem(gy + p, GY)
        here = obs_all.at[:, :, pl.ds(pl.multiple_of(base * LANES, SLOTS * LANES), SLOTS * LANES)]
        return remote(here, here, qsend.at[to], qrecv.at[gy], {"space": to * SLOTS + slot})

    def column_wait(p):
        of = lax.rem(gy + p, GY)
        here = obs_all.at[:, :, pl.ds(pl.multiple_of(of * SLOTS * LANES, SLOTS * LANES), SLOTS * LANES)]
        remote(here, here, qsend.at[of], qrecv.at[of], {"space": of * SLOTS + slot}).wait_recv()

    def over_four(body):
        def at(p, carry):
            body(p)
            return carry

        lax.fori_loop(1, 4, at, 0)

    lane_ids = lax.broadcasted_iota(jnp.int32, (1, LANES), 1)

    def live_at(j, carry):
        live[:, pl.ds(pl.multiple_of(j * LANES, LANES), LANES)] = jnp.where(lane_ids < counts[j], 1.0, 0.0)
        return carry

    lax.fori_loop(0, GY * SLOTS, live_at, 0)

    core_rows = pl.ds(TOP, BY)

    def edge_layer(x):
        v[:, :, x, core_rows] = jnp.zeros((2, 2, BY, LANES), F32)

    def edge_rows(side):
        yrecv[:, side] = jnp.zeros((2, 2, BX, LANES), F32)

    pl.when(gy == 0)(lambda: edge_layer(0))
    pl.when(gy == GY - 1)(lambda: edge_layer(BX + 1))
    pl.when(gx == 0)(lambda: edge_rows(0))
    pl.when(gx == GX - 1)(lambda: edge_rows(1))

    def halo(at):
        up = {"space": space - SLOTS}
        down = {"space": space + SLOTS}
        left = {"space": space - 2}
        right = {"space": space + 2}
        return (
            (gy > 0, gy < GY - 1,
             remote(v.at[at, :, 1, core_rows], v.at[at, :, BX + 1, core_rows], hsend.at[at, 0], hrecv.at[at, 0], up)),
            (gy < GY - 1, gy > 0,
             remote(v.at[at, :, BX, core_rows], v.at[at, :, 0, core_rows], hsend.at[at, 1], hrecv.at[at, 1], down)),
            (gx > 0, gx < GX - 1,
             remote(ysend.at[at, 0], yrecv.at[at, 1], hsend.at[at, 2], hrecv.at[at, 2], left)),
            (gx < GX - 1, gx > 0,
             remote(ysend.at[at, 1], yrecv.at[at, 0], hsend.at[at, 3], hrecv.at[at, 3], right)),
        )

    def exchange(at):
        copies = halo(at)
        for sends, _, copy in copies:
            pl.when(sends)(copy.start)
        for sends, takes, copy in copies:
            pl.when(takes)(copy.wait_recv)
            pl.when(sends)(copy.wait_send)

    def put(at, half, x, value):
        v[at, half, x + 1, TOP : TOP + BY, :] = value
        ysend[at, 0, half, pl.ds(x, 1), :] = value[0:1]
        ysend[at, 1, half, pl.ds(x, 1), :] = value[BY - 1 : BY]

    lane = lax.broadcasted_iota(jnp.int32, (BY, LANES), 1)

    def over_x(body, unroll=1):
        def at(x, carry):
            body(x)
            return carry

        lax.fori_loop(0, BX, at, 0, unroll=unroll)

    def neighbour_sums(at, x):
        c0 = v[at, 0, x + 1, TOP : TOP + BY, :]
        c1 = v[at, 1, x + 1, TOP : TOP + BY, :]
        next0, next1 = pltpu.roll(c0, LANES - 1, 1), pltpu.roll(c1, LANES - 1, 1)
        last0, last1 = pltpu.roll(c0, 1, 1), pltpu.roll(c1, 1, 1)
        z0 = jnp.where(lane == LANES - 1, next1, next0) + jnp.where(lane == 0, 0.0, last0)
        z1 = jnp.where(lane == LANES - 1, 0.0, next1) + jnp.where(lane == 0, last0, last1)
        sums = []
        for half, z in ((0, z0), (1, z1)):
            total = v[at, half, x + 2, TOP : TOP + BY, :] + v[at, half, x, TOP : TOP + BY, :]
            total = total + v[at, half, x + 1, TOP + 1 : TOP + BY + 1, :] + v[at, half, x + 1, TOP - 1 : TOP + BY - 1, :]
            sums.append(total + z)
        return sums

    def spread_rows(at):
        def body(x):
            for half in range(2):
                v[at, half, x + 1, TOP - 1 : TOP, :] = yrecv[at, 0, half, pl.ds(x, 1), :]
                v[at, half, x + 1, TOP + BY : TOP + BY + 1, :] = yrecv[at, 1, half, pl.ds(x, 1), :]

        over_x(body, unroll=4)

    def locate(sign, k):
        cells = dip[sign : sign + 1, pl.ds(pl.multiple_of(k * CHUNK, CHUNK), CHUNK)]
        x, y, z = cells >> 15, (cells >> 8) & 127, cells & 255
        own = ((x >> 4) == gy) & ((y >> 5) == gx)
        row = jnp.where(own, (x & 15) * BY + (y & 31), -1)
        hot = lax.broadcasted_iota(jnp.int32, (ROWS, CHUNK), 0) == row
        return jnp.where(hot, 1.0, 0.0).astype(BF16), lax.broadcasted_iota(jnp.int32, (2 * LANES, CHUNK), 0) == z

    def gather(n):
        for half in range(2):
            rows = un[n, half].reshape(ROWS, LANES).T
            high = rows.astype(BF16)
            ut[half * LANES : (half + 1) * LANES, :] = high
            ut[(2 + half) * LANES : (3 + half) * LANES, :] = (rows - high.astype(F32)).astype(BF16)

        def at(k, carry):
            found = []
            for sign in range(2):
                hot, depth = locate(sign, k)
                both = jnp.dot(ut[...], hot, preferred_element_type=F32)
                value = both[: 2 * LANES] + both[2 * LANES :]
                found.append(jnp.sum(jnp.where(depth, value, 0.0), axis=0, keepdims=True))
            part[n, :, pl.ds(pl.multiple_of(k * CHUNK, CHUNK), CHUNK)] = found[0] - found[1]
            return carry

        lax.fori_loop(0, NDIP // CHUNK, at, 0)

    def scatter(n):
        acc[...] = jnp.zeros_like(acc)

        def at(k, carry):
            value = res[n, :, pl.ds(pl.multiple_of(k * CHUNK, CHUNK), CHUNK)]
            for sign in range(2):
                hot, depth = locate(sign, k)
                placed = jnp.where(depth, value if sign == 0 else -value, 0.0)
                high = placed.astype(BF16)
                low = (placed - high.astype(F32)).astype(BF16)
                acc[...] += lax.dot_general(
                    hot, jnp.concatenate([high, low], axis=0), (((1,), (1,)), ((), ())), preferred_element_type=F32
                )
            return carry

        lax.fori_loop(0, NDIP // CHUNK, at, 0)

    def injected(half, x):
        rows = pl.ds(pl.multiple_of(x * BY, BY), BY)
        return (
            acc[rows, half * LANES : (half + 1) * LANES] + acc[rows, (2 + half) * LANES : (3 + half) * LANES]
        )

    take_field(U0)

    def begin(x):
        for half in range(2):
            put(0, half, x, blk[U0, half, x])

    over_x(begin)
    take_static(COND)
    take_field(R0)

    def step_zero(x):
        for half in range(2):
            inv[half, x] = 1.0 / (6.0 + sblk[COND, half, x])
            rhs[half, x] = blk[R0, half, x]

    over_x(step_zero)

    def forward_sweep(s, carry):
        at = lax.rem(s, 2)
        exchange(at)
        spread_rows(at)

        def body(x):
            sums = neighbour_sums(at, x)
            for half in range(2):
                put(1 - at, half, x, (rhs[half, x] + sums[half]) * inv[half, x])

        over_x(body, unroll=2)
        return carry

    def keep(n):
        def body(x):
            for half in range(2):
                un[n, half, x] = v[0, half, x + 1, TOP : TOP + BY, :]

        over_x(body)

    def statics(x):
        for half in range(2):
            c, g = sblk[COND, half, x], sblk[CHG, half, x]
            rate = 1.0 / sblk[RLX, half, x]
            a0, a1, e1, b0, b1 = (jnp.zeros((BY, LANES), F32) for _ in range(5))
            for k in range(4):
                decay = jnp.exp(-rate / RATIOS[k])
                fresh = WEIGHTS[k] * (1.0 - decay)
                a0 = a0 + fresh
                a1 = a1 + fresh * decay
                tilt = decay * (WEIGHTS[k] / RATIOS[k])
                b0 = b0 + tilt
                b1 = b1 + tilt * (1.0 - 2.0 * decay)
            f1[half, x] = c * g * a0
            f2[half, x] = c * g * a1
            ka0[half, x] = c * a0
            ka1[half, x] = c * a1
            kb0[half, x] = c * g * rate * rate * b0
            kb1[half, x] = c * g * rate * rate * b1

    for n in range(NSTEPS):
        lax.fori_loop(0, JACOBI, forward_sweep, 0)
        keep(n)
        if n == 0:
            take_static(CHG)
            take_static(RLX)
            over_x(statics)
            take_field(R1)

            def step_one(x):
                for half in range(2):
                    rhs[half, x] = blk[R1, half, x] + f1[half, x] * un[0, half, x]

            over_x(step_one)
            over_peers(obs_wait)
            over_four(lambda p: column_copy(p).start())
        if n == 1:
            take_field(R2)

            def step_two(x):
                for half in range(2):
                    rhs[half, x] = (
                        blk[R2, half, x] + f2[half, x] * un[0, half, x] + f1[half, x] * un[1, half, x]
                    )

            over_x(step_two)
            over_four(column_wait)
        gather(n)

    def row_copy(p):
        to = lax.rem(gx + p, GX)
        return remote(part, prx.at[gx], psend.at[0, to], precv.at[0, gx], {"space": base + 2 * to + core})

    def row_wait(p):
        of = lax.rem(gx + p, GX)
        remote(part, prx.at[of], psend.at[0, of], precv.at[0, of], {"space": base + 2 * of + core}).wait_recv()

    over_four(lambda p: row_copy(p).start())
    prx[gx] = part[...]
    over_four(row_wait)
    res[...] = (prx[0] + prx[1]) + (prx[2] + prx[3])

    def col_copy(p):
        to = lax.rem(gy + p, GY)
        return remote(res, pry.at[gy], psend.at[1, to], precv.at[1, gy], {"space": to * SLOTS + slot})

    def col_wait(p):
        of = lax.rem(gy + p, GY)
        remote(res, pry.at[of], psend.at[1, of], precv.at[1, of], {"space": of * SLOTS + slot}).wait_recv()

    over_four(lambda p: col_copy(p).start())
    pry[gy] = res[...]
    over_four(col_wait)
    over_four(lambda p: col_copy(p).wait_send())
    squares = jnp.zeros((1, NDIP), F32)
    for n in range(NSTEPS):
        volts = live[...] * ((pry[0, n] + pry[1, n]) + (pry[2, n] + pry[3, n]))
        part_resid = live[...] * (volts - obs_all[n])
        pry[0, n] = volts
        res[n] = part_resid
        squares = squares + part_resid * part_resid

    own = pl.ds(pl.multiple_of(space * LANES, LANES), LANES)
    other = pl.ds(pl.multiple_of(partner * LANES, LANES), LANES)
    swap = remote(pry.at[0, :, :, other], vswap.at[pl.ds(6, 3)], qsend.at[4], qrecv.at[4], {"space": partner})
    swap.start()
    lanes = squares[:, 0:LANES]
    for j in range(1, NDIP // LANES):
        lanes = lanes + squares[:, j * LANES : (j + 1) * LANES]
    sq[...] = lanes
    pair = remote(sq, sqc, qsend.at[5], qrecv.at[5], {"space": partner})
    pair.start()
    for n in range(NSTEPS):
        volts_out[n, pl.ds(core, 1), :] = pry[0, n, :, own]
    swap.wait()
    for n in range(NSTEPS):
        volts_out[n, pl.ds(1 - core, 1), :] = vswap[6 + n]
    pair.wait()
    sqz[tx] = sq[...] + sqc[...]

    def sq_copy(p):
        to = lax.rem(tx + p, 4)
        return remote(sqz.at[tx], sqz.at[tx], gsend.at[3, to], grecv.at[3, tx], {"tx": to})

    def sq_wait(p):
        of = lax.rem(tx + p, 4)
        remote(sqz.at[of], sqz.at[of], gsend.at[3, of], grecv.at[3, of], {"tx": of}).wait_recv()

    over_four(lambda p: sq_copy(p).start())

    def begin_adjoint(n):
        def body(x):
            for half in range(2):
                field = injected(half, x)
                if n == 1:
                    field = field + back[half, x] + f1[half, x] * adj[2, half, x]
                scaled = field * inv[half, x]
                adj[n, half, x] = scaled
                put(0, half, x, scaled)

        over_x(body)

    def adjoint_sweep(n, s, carry):
        at = lax.rem(s, 2)
        exchange(at)
        spread_rows(at)

        def body(x):
            sums = neighbour_sums(at, x)
            for half in range(2):
                scaled = sums[half] * inv[half, x]
                adj[n, half, x] += scaled
                put(1 - at, half, x, scaled)

        over_x(body, unroll=2)
        return carry

    scatter(2)
    begin_adjoint(2)
    lax.fori_loop(0, JACOBI - 1, functools.partial(adjoint_sweep, 2), 0)
    exchange((JACOBI - 1) % 2)
    spread_rows((JACOBI - 1) % 2)

    def last_back(x):
        sums = neighbour_sums((JACOBI - 1) % 2, x)
        for half in range(2):
            back[half, x] = sums[half]

    over_x(last_back)
    scatter(1)
    begin_adjoint(1)
    lax.fori_loop(0, JACOBI - 1, functools.partial(adjoint_sweep, 1), 0)

    over_four(sq_wait)
    total = (sqz[0] + sqz[1]) + (sqz[2] + sqz[3])
    misfit = jnp.sqrt(1.0 + jnp.sum(total, axis=1, keepdims=True))
    misfit_out[...] = misfit
    take_field(T1)
    take_field(T2)

    def gradients(i, carry):
        x = i
        row, rest = x // 4, lax.rem(x, 4)
        side, layer = rest // 2, lax.rem(rest, 2)
        for half in range(2):
            s1, s2 = adj[1, half, x], adj[2, half, x]
            u0, u1 = un[0, half, x], un[1, half, x]
            same = s2 * u1 + s1 * u0
            cross = s2 * u0
            grad[0, row, side, half, layer] = ka0[half, x] * same + ka1[half, x] * cross
            grad[1, row, side, half, layer] = (
                s1 * blk[T1, half, x] + s2 * blk[T2, half, x] - kb0[half, x] * same + kb1[half, x] * cross
            )
        return carry

    lax.fori_loop(0, BX, gradients, 0)
    across = remote(grad.at[:, :, 1 - core], rc, gsend.at[2, 0], grecv.at[2, 0], {"space": partner})
    across.start()
    across.wait()

    def sum_cores(i, carry):
        f, row = i // 4, lax.rem(i, 4)
        red[f, row] = grad[f, row, core] + rc[f, row]
        return carry

    lax.fori_loop(0, 8, sum_cores, 0)

    def back_copy(p):
        to = lax.rem(gx + p, GX)
        return remote(red.at[:, to], rx.at[:, gx], gsend.at[0, to], grecv.at[0, gx], {"space": base + 2 * to + core})

    def back_wait(p):
        of = lax.rem(gx + p, GX)
        remote(red.at[:, of], rx.at[:, of], gsend.at[0, of], grecv.at[0, of], {"space": base + 2 * of + core}).wait_recv()

    over_four(lambda p: back_copy(p).start())
    for f in range(2):
        rx[f, gx] = red[f, gx]
    over_four(back_wait)

    def tx_copy(p):
        to = lax.rem(tx + p, 4)
        return remote(rx.at[:, to], rz.at[:, tx], gsend.at[1, to], grecv.at[1, tx], {"tx": to})

    def tx_wait(p):
        of = lax.rem(tx + p, 4)
        remote(rx.at[:, of], rz.at[:, of], gsend.at[1, of], grecv.at[1, of], {"tx": of}).wait_recv()

    over_four(lambda p: tx_copy(p).start())
    for f in range(2):
        rz[f, tx] = rx[f, tx]
    over_four(tx_wait)
    scale = 1.0 / misfit
    for f, out in ((0, gc_out), (1, gt_out)):
        for half in range(2):
            value = (rz[f, 0, half] + rz[f, 1, half]) + (rz[f, 2, half] + rz[f, 3, half])
            out[:, :, half * LANES : (half + 1) * LANES] = value * scale.reshape(1, 1, 1)

    for f in range(6):
        over_peers(lambda p: field_copy(f, p).wait_send())
    for f in range(3):
        over_peers(lambda p: static_copy(f, p).wait_send())
    over_peers(lambda p: obs_copy(p).wait_send())
    over_four(lambda p: column_copy(p).wait_send())
    over_four(lambda p: row_copy(p).wait_send())
    over_four(lambda p: sq_copy(p).wait_send())
    over_four(lambda p: back_copy(p).wait_send())
    over_four(lambda p: tx_copy(p).wait_send())


def on_device(cond, chg, rlx, start, mem, src_cells, dip, counts, obs):
    vmem = pl.BlockSpec(memory_space=pltpu.VMEM)
    smem = pl.BlockSpec(memory_space=pltpu.SMEM)
    field = pltpu.VMEM((2, BX, BY, LANES), F32)
    dma = pltpu.SemaphoreType.DMA
    scratch = [
        pltpu.VMEM((6, 2, GX, 2, 2, BY, LANES), F32),
        pltpu.VMEM((3, GX, 2, 2, BY, LANES), F32),
        pltpu.VMEM((6, 2, BX, BY, LANES), F32),
        pltpu.VMEM((3, 2, BX, BY, LANES), F32),
        pltpu.VMEM((2, 2, BX + 2, BY + 2 * TOP, LANES), F32),
        pltpu.VMEM((2, 2, 2, BX, LANES), F32),
        pltpu.VMEM((2, 2, 2, BX, LANES), F32),
        field, field, field, field, field, field, field, field,
        pltpu.VMEM((NSTEPS, 2, BX, BY, LANES), F32),
        pltpu.VMEM((NSTEPS, 2, BX, BY, LANES), F32),
        field,
        pltpu.VMEM((4 * LANES, ROWS), BF16),
        pltpu.VMEM((ROWS, 4 * LANES), F32),
        pltpu.VMEM((NSTEPS, 1, NDIP), F32),
        pltpu.VMEM((GX, NSTEPS, 1, NDIP), F32),
        pltpu.VMEM((GY, NSTEPS, 1, NDIP), F32),
        pltpu.VMEM((NSTEPS, 1, NDIP), F32),
        pltpu.VMEM((NSTEPS, 1, NDIP), F32),
        pltpu.VMEM((1, NDIP), F32),
        pltpu.VMEM((9, 1, LANES), F32),
        pltpu.VMEM((1, LANES), F32),
        pltpu.VMEM((1, LANES), F32),
        pltpu.VMEM((4, 1, LANES), F32),
        pltpu.VMEM((2, GX, 2, 2, 2, BY, LANES), F32),
        pltpu.VMEM((2, GX, 2, 2, BY, LANES), F32),
        pltpu.VMEM((2, GX, 2, 2, BY, LANES), F32),
        pltpu.VMEM((2, GX, 2, 2, BY, LANES), F32),
        pltpu.VMEM((2, 4, 2, 2, BY, LANES), F32),
        dma((6, SLOTS)), dma((6, SLOTS)), dma((3, SLOTS)), dma((3, SLOTS)),
        dma((2, 4)), dma((2, 4)),
        dma((SLOTS,)), dma((SLOTS,)),
        dma((2, 4)), dma((2, 4)),
        dma((6,)), dma((6,)),
        dma((4, 4)), dma((4, 4)),
    ]
    volts, misfit, grad_c, grad_t = pl.pallas_call(
        kernel,
        out_shape=(
            jax.ShapeDtypeStruct((NSTEPS, 2, LANES), F32),
            jax.ShapeDtypeStruct((1, 1), F32),
            jax.ShapeDtypeStruct((2, BY, 2 * LANES), F32),
            jax.ShapeDtypeStruct((2, BY, 2 * LANES), F32),
        ),
        in_specs=[vmem, vmem, vmem, vmem, vmem, smem, vmem, smem, vmem],
        out_specs=(vmem, vmem, vmem, vmem),
        scratch_shapes=scratch,
        compiler_params=pltpu.CompilerParams(has_side_effects=True, vmem_limit_bytes=56 << 20),
    )(cond, chg, rlx, start, mem, src_cells, dip, counts, obs)
    return (volts, misfit.reshape(()), grad_c, grad_t)


def solution(mesh):
    placed = (
        P("space", None, None),
        P("space", None, None),
        P("space", None, None),
        P("tx", "space", None, None),
        P(None, "tx", "space", None, None),
        P(None, "tx"),
        P(),
        P(),
        P(None, "tx", "space"),
    )
    return jax.shard_map(
        on_device,
        mesh=mesh,
        in_specs=placed,
        out_specs=(P(None, "tx", "space"), P(), P("space", "tx", None), P("space", "tx", None)),
        check_vma=False,
    )
```

time: 1170 us -> 312 us (0.27); the launches traced: 1150 us -> 309 us
  starting transfers between devices: 319 us -> 0 us
  Pallas kernels: 0 us -> 302 us
  waiting for transfers between devices: 249 us -> 0 us
  local copies, waits for them, and re-layouts: 248 us -> 4.21 us
  other arithmetic: 224 us -> 0 us
  blocking collectives: 97.2 us -> 0 us
  between operations: 18 us -> 2.4 us
    ppermute x78 -> x0, starting transfers between devices: 319 us -> none  [the longest x39 238 us: extended(): after = lax.ppermute(initial, axis, down)]
    pallas_call x0 -> x1, Pallas kernels: none -> 302 us  [on_device(): pl.pallas_call(kernel, out_shape=(jax.ShapeDtypeStruct((NSTEPS, 2, LANES)...]
    scatter-add x6 -> x0, other arithmetic: 167 us -> none  [the longest x2 90.1 us: on_device(): inject.at[:, probe_two].add(-spread[step] * inside_two)]
    gather x6 -> x0, local copies, waits for them, and re-layouts: 148 us -> none  [the longest x3 74.2 us: on_device(): jnp.take(flat, probe_one, axis=1) * inside_one]
    reduce_scatter x3 -> x0, waiting for transfers between devices: 134 us -> none  [the longest x1 86.8 us: on_device(): lax.psum_scatter(jnp.stack(partials), 'space', scatter_dimension=2, tiled...]
    ppermute x78 -> x0, waiting for transfers between devices: 115 us -> none  [the longest x39 106 us: extended(): before = lax.ppermute(last, axis, up)]
    psum x1 -> x0, blocking collectives: 64.8 us -> none  [total_misfit(): return jnp.sqrt(1.0 + lax.psum(partial_value, ('space', 'tx')))]
    mul x3 -> x0, local copies, waits for them, and re-layouts: 51.4 us -> none  [on_device(): forward_field = (rhs + neighbours(rim_one(forward_field))) * inverse]
  transfers between devices with their start and end apart: 81 -> 0, of which waited for: 46 -> 0; matrix products, arithmetic and copies ran while one was open for 22% -> 0% of each run, Pallas kernels for 0% -> 0%
where the time goes in v1:
time: 312 us; the launch traced here: 309 us
  Pallas kernels  302 us (97%)
  local copies, waits for them, and re-layouts  4.21 us (1%)
    pallas_call x1, Pallas kernels, on_device(): pl.pallas_call(kernel, out_shape=(jax.ShapeDtypeStruct((NSTEPS, 2, LANES)...  302 us

profile of v1, /device:TPU:19, one launch (start us, length us, event | category | flops | bytes accessed | tf_op | source)
XLA Modules:
  0.0 308.6 jit_solution(2626375786770615313)
XLA Ops:
  0.6 302.0 %shard_map.120 = (f32[3,2,128]{2,1,0:T(2,128)}, f32[1,1]{1,0:T(1,128)}, f32[2,32,256]{2,1,0:T(8,128)}, f32[2,32,256]{2,1,0:T(8,128)}) custom-call(f32[2,128,256]{2,1,0:T(8,128)} %cond.1, f32[2,128,256]{2,1,0:T(8,128)} %chg.1, f32[2,128,256]{2,1,0:T(8,128)} %rlx.1, f32[2,2,128,256]{3,2,1,0:T(8,128)} %start.1, f32[4,2,2,128,256]{4,3,2,1,0:T(8,128)} %mem.1, ...), custom_call_target="tpu_custom_call" | custom-call | tf_op jit(solution)/shard_map/pallas_call | solution.py:628
  302.6 1.3 copy.17
  304.5 1.5 copy.19
  306.0 1.5 copy.20

commit v2 on v1

v2 whole, which is shorter than its diff:
```python
import functools

import jax
import jax.numpy as jnp
from jax import lax
from jax.experimental import pallas as pl
from jax.experimental.pallas import tpu as pltpu
from jax.sharding import PartitionSpec as P

MESH = pl.DeviceIdType.MESH
F32 = jnp.float32
BF16 = jnp.bfloat16
NSTEPS = 3
JACOBI = 8
WEIGHTS = (0.4, 0.3, 0.2, 0.1)
RATIOS = (0.25, 1.0, 4.0, 16.0)
STRENGTH = 4.0

NB, NXB = 4, 4
SLOTS = 8
BX, BY, LANES = 16, 32, 128
HALO = 8
EX, EY = BX + 2 * HALO, BY + 2 * HALO
PAD = 8
VTOP = PAD + HALO
NDIP = 4096
CHUNK = 512
ROWS = BX * BY
UNROLL = 4
R1, R2, T1, T2 = range(4)
COND, CHG, RLX = range(3)
U0, R0 = 4, 5
SIDES = tuple((i, j) for i in (-1, 0, 1) for j in (-1, 0, 1) if (i, j) != (0, 0))


def remote(src, dst, send, recv, device):
    return pltpu.make_async_remote_copy(
        src_ref=src, dst_ref=dst, send_sem=send, recv_sem=recv, device_id=device, device_id_type=MESH
    )


def kernel(
    cond, chg, rlx, start, mem, src_cells, dip, counts, obs,
    volts_out, misfit_out, gc_out, gt_out,
    stage, sstage, blk, sblk, entry, va, vb,
    inv, rhs, f1, f2, ka0, ka1, kb0, kb1, ulast, adj, back,
    ut, acc, part, prx, pry, res, obs_all, live, vswap, sq, sqc, sqz,
    grad, rx, rsum, rz,
    fsend, frecv, ssend, srecv, hsend, hrecv, osend, orecv, psend, precv, qsend, qrecv, gsend, grecv, tsend, trecv,
):
    space = lax.axis_index("space")
    tx = lax.axis_index("tx")
    yp = space // SLOTS
    slot = lax.rem(space, SLOTS)
    gx = slot // 2
    mine = lax.rem(yp, 2)
    bx = 2 * (yp // 2) + lax.rem(slot, 2)
    partner = (yp + 1 - 2 * mine) * SLOTS + slot

    def device(b, x, t):
        return (2 * (b // 2) + t) * SLOTS + 2 * x + lax.rem(b, 2)

    def over(count, body, first=0):
        def at(p, carry):
            body(p)
            return carry

        lax.fori_loop(first, count, at, 0)

    def pieces(body):
        def at(i, carry):
            row, layer = i // 2, lax.rem(i, 2)
            for half in range(2):
                body(row, layer, half, (layer, pl.ds(pl.multiple_of(row * BY, BY), BY), pl.ds(half * LANES, LANES)))
            return carry

        lax.fori_loop(0, 2 * NXB, at, 0)

    def first_fields(row, layer, half, where):
        c = cond[where]
        sstage[COND, row, half, layer] = c
        ids = (2 * space + layer) * (128 * 256) + row * (BY * 256) + half * LANES
        ids = ids + lax.broadcasted_iota(jnp.int32, (BY, LANES), 0) * 256
        ids = ids + lax.broadcasted_iota(jnp.int32, (BY, LANES), 1)
        for t in range(2):
            stage[U0, t, row, half, layer] = start[(t,) + where]
            total = mem[(0, t) + where] + mem[(1, t) + where] + mem[(2, t) + where] + mem[(3, t) + where]
            source = jnp.where(ids == src_cells[0, t], STRENGTH, 0.0) - jnp.where(ids == src_cells[1, t], STRENGTH, 0.0)
            stage[R0, t, row, half, layer] = source + c * total

    def later_fields(row, layer, half, where):
        c = cond[where]
        relax = rlx[where]
        sstage[CHG, row, half, layer] = chg[where]
        sstage[RLX, row, half, layer] = relax
        rate = 1.0 / relax
        decays = [jnp.exp(-rate / ratio) for ratio in RATIOS]
        for t in range(2):
            first, second, slope, slope_d = (jnp.zeros((BY, LANES), F32) for _ in range(4))
            for k in range(4):
                scaled = decays[k] * mem[(k, t) + where]
                first = first + scaled
                second = second + decays[k] * scaled
                tilt = scaled * (1.0 / RATIOS[k])
                slope = slope + tilt
                slope_d = slope_d + decays[k] * tilt
            stage[R1, t, row, half, layer] = c * first
            stage[R2, t, row, half, layer] = c * second
            stage[T1, t, row, half, layer] = c * rate * rate * slope
            stage[T2, t, row, half, layer] = 2.0 * c * rate * rate * slope_d

    def landing(f, j):
        layers = pl.ds(HALO + 2 * j, 2)
        if f == U0:
            return entry.at[0, :, layers, pl.ds(VTOP, BY)]
        if f == R0:
            return rhs.at[0, :, layers, pl.ds(HALO, BY)]
        return blk.at[f, :, pl.ds(2 * j, 2)]

    def target(p):
        q = lax.rem(p + slot, SLOTS)
        return q // 2, lax.rem(q, 2), q, device(yp, q // 2, lax.rem(q, 2))

    def field_copy(f, p):
        x, t, q, to = target(p)
        return to, remote(stage.at[f, t, x], landing(f, slot), fsend.at[f, q], frecv.at[f, slot], {"space": to})

    def static_copy(f, p):
        x, t, q, to = target(p)
        return to, remote(sstage.at[f, x], sblk.at[f, :, pl.ds(2 * slot, 2)], ssend.at[f, q], srecv.at[f, slot], {"space": to})

    def begin(f, copy_of):
        def one(p):
            to, copy = copy_of(f, p)
            pl.when(to != space)(copy.start)

        over(SLOTS, one)

    def finish(f, copy_of):
        def one(p):
            to, copy = copy_of(f, p)
            pl.when(to != space)(copy.wait_send)

        over(SLOTS, one)

    def send_field(f):
        begin(f, field_copy)

        def keep():
            if f == U0:
                entry[0, :, pl.ds(HALO + 2 * slot, 2), VTOP : VTOP + BY] = stage[f, mine, gx]
            elif f == R0:
                rhs[0, :, pl.ds(HALO + 2 * slot, 2), HALO : HALO + BY] = stage[f, mine, gx]
            else:
                blk[f, :, pl.ds(2 * slot, 2)] = stage[f, mine, gx]

        pl.when(bx == yp)(keep)

    def send_static(f):
        begin(f, static_copy)

        def keep():
            sblk[f, :, pl.ds(2 * slot, 2)] = sstage[f, gx]

        pl.when(bx == yp)(keep)

    def take_field(f):
        def one(j):
            here = landing(f, j)
            of = bx * SLOTS + j
            copy = remote(here, here, fsend.at[f, j], frecv.at[f, j], {"space": of})
            pl.when(of != space)(copy.wait_recv)

        over(SLOTS, one)

    def take_static(f):
        def one(j):
            here = sblk.at[f, :, pl.ds(2 * j, 2)]
            of = bx * SLOTS + j
            copy = remote(here, here, ssend.at[f, j], srecv.at[f, j], {"space": of})
            pl.when(of != space)(copy.wait_recv)

        over(SLOTS, one)

    pieces(first_fields)
    send_field(U0)
    send_field(R0)
    send_static(COND)

    def clear(ref, index):
        shape = ref.at[index].shape
        ref[index] = jnp.zeros(shape, F32)

    def clear_pads(x):
        for ref in (va, vb):
            for half in range(2):
                clear(ref, (half, x, pl.ds(0, PAD)))
                clear(ref, (half, x, pl.ds(PAD + EY, PAD)))
        for k in range(5):
            for half in range(2):
                clear(entry, (k, half, x, pl.ds(0, PAD)))
                clear(entry, (k, half, x, pl.ds(PAD + EY, PAD)))

    over(EX, clear_pads)

    def clear_rows(low):
        def one(x):
            for half in range(2):
                at = 0 if low else HALO + BY
                for k in range(5):
                    clear(entry, (k, half, x, pl.ds(PAD + at, HALO)))
                for n in range(NSTEPS):
                    clear(rhs, (n, half, x, pl.ds(at, HALO)))
                clear(inv, (half, x, pl.ds(at, HALO)))

        over(EX, one)

    def clear_layers(low):
        def one(i):
            x = i if low else i + HALO + BX
            for half in range(2):
                for k in range(5):
                    clear(entry, (k, half, x, pl.ds(PAD, EY)))
                for n in range(NSTEPS):
                    clear(rhs, (n, half, x))
                clear(inv, (half, x))

        over(HALO, one)

    pl.when(gx == 0)(lambda: clear_rows(True))
    pl.when(gx == NXB - 1)(lambda: clear_rows(False))
    pl.when(bx == 0)(lambda: clear_layers(True))
    pl.when(bx == NB - 1)(lambda: clear_layers(False))

    def slab_lanes(s, count=1):
        return pl.ds(pl.multiple_of(s * LANES, LANES), count * LANES)

    for t in range(2):
        for n in range(NSTEPS):
            vswap[3 * t + n] = obs[n, t : t + 1, :]
    obs_pair = remote(
        vswap.at[pl.ds(3 * (1 - mine), 3)], obs_all.at[:, :, slab_lanes(space)], qsend.at[0], qrecv.at[0], {"space": partner}
    )
    obs_pair_in = remote(
        vswap.at[pl.ds(3 * (1 - mine), 3)], obs_all.at[:, :, slab_lanes(partner)], qsend.at[0], qrecv.at[0], {"space": partner}
    )
    obs_pair.start()
    obs_all[:, :, slab_lanes(space)] = vswap[pl.ds(3 * mine, 3)]

    def obs_copy(p, which):
        to = lax.rem(slot + p, SLOTS)
        here = obs_all.at[:, :, slab_lanes(space if which == 0 else partner)]
        return remote(here, here, osend.at[which, to], orecv.at[which, slot], {"space": yp * SLOTS + to})

    def obs_wait(p, which):
        of = lax.rem(slot + p, SLOTS)
        row = yp if which == 0 else yp + 1 - 2 * mine
        here = obs_all.at[:, :, slab_lanes(row * SLOTS + of)]
        remote(here, here, osend.at[which, of], orecv.at[which, of], {"space": yp * SLOTS + of}).wait_recv()

    def obs_rows(own):
        half = yp // 2 if own else 1 - yp // 2
        here = obs_all.at[:, :, slab_lanes(2 * half * SLOTS, 2 * SLOTS)]
        return remote(here, here, qsend.at[1], qrecv.at[1], {"space": lax.rem(space + 2 * SLOTS, NB * SLOTS)})

    lane_ids = lax.broadcasted_iota(jnp.int32, (1, LANES), 1)

    def live_at(j, carry):
        live[:, pl.ds(pl.multiple_of(j * LANES, LANES), LANES)] = jnp.where(lane_ids < counts[j], 1.0, 0.0)
        return carry

    lax.fori_loop(0, NB * SLOTS, live_at, 0)

    def halo(ref, top, which):
        copies = []
        for side, (i, j) in enumerate(SIDES):
            layers = {-1: (HALO, HALO, HALO + BX), 1: (BX, HALO, 0), 0: (HALO, BX, HALO)}[i]
            rows = {-1: (top, HALO, top + BY), 1: (top + BY - HALO, HALO, top - HALO), 0: (top, BY, top)}[j]
            sends = (bx + i >= 0) & (bx + i < NB) & (gx + j >= 0) & (gx + j < NXB)
            takes = (bx - i >= 0) & (bx - i < NB) & (gx - j >= 0) & (gx - j < NXB)
            to = device(lax.rem(bx + i + NB, NB), lax.rem(gx + j + NXB, NXB), mine)
            copies.append((sends, takes, remote(
                ref.at[:, pl.ds(layers[0], layers[1]), pl.ds(rows[0], rows[1])],
                ref.at[:, pl.ds(layers[2], layers[1]), pl.ds(rows[2], rows[1])],
                hsend.at[which, side], hrecv.at[which, side], {"space": to},
            )))
        return copies

    def halo_start(ref, top, which):
        for sends, _, copy in halo(ref, top, which):
            pl.when(sends)(copy.start)

    def halo_wait(ref, top, which):
        for sends, takes, copy in halo(ref, top, which):
            pl.when(takes)(copy.wait_recv)
            pl.when(sends)(copy.wait_send)

    def over_x(body, unroll=1):
        def at(x, carry):
            body(x)
            return carry

        lax.fori_loop(0, BX, at, 0, unroll=unroll)

    def neighbour_sums(ref, x, top, rows):
        c0 = ref[0, x, top : top + rows]
        c1 = ref[1, x, top : top + rows]
        lane = lax.broadcasted_iota(jnp.int32, (rows, LANES), 1)
        next0, next1 = pltpu.roll(c0, LANES - 1, 1), pltpu.roll(c1, LANES - 1, 1)
        last0, last1 = pltpu.roll(c0, 1, 1), pltpu.roll(c1, 1, 1)
        z0 = jnp.where(lane == LANES - 1, next1, next0) + jnp.where(lane == 0, 0.0, last0)
        z1 = jnp.where(lane == LANES - 1, 0.0, next1) + jnp.where(lane == 0, last0, last1)
        sums = []
        for half, z in ((0, z0), (1, z1)):
            total = ref[half, x + 1, top : top + rows] + ref[half, x - 1, top : top + rows]
            total = total + ref[half, x, top + 1 : top + rows + 1] + ref[half, x, top - 1 : top + rows - 1]
            sums.append(total + z)
        return sums

    def sweeps(first, last, body, closing):
        source = first
        for s in range(1, last + 1):
            goal = va if s % 2 else vb
            if s == HALO:
                def one(x, carry, source=source):
                    closing(x, neighbour_sums(source, x, VTOP, BY))
                    return carry
            else:
                def one(x, carry, source=source, goal=goal):
                    sums = neighbour_sums(source, x, PAD, EY)
                    for half in range(2):
                        goal[half, x, PAD : PAD + EY] = body(half, x, sums[half])
                    return carry
            lax.fori_loop(s, EX - s, one, 0, unroll=UNROLL)
            source = goal

    def locate(sign, k):
        cells = dip[sign : sign + 1, pl.ds(pl.multiple_of(k * CHUNK, CHUNK), CHUNK)]
        x, y, z = cells >> 15, (cells >> 8) & 127, cells & 255
        own = ((x >> 4) == bx) & ((y >> 5) == gx)
        row = jnp.where(own, (x & 15) * BY + (y & 31), -1)
        hot = lax.broadcasted_iota(jnp.int32, (ROWS, CHUNK), 0) == row
        return jnp.where(hot, 1.0, 0.0).astype(BF16), lax.broadcasted_iota(jnp.int32, (2 * LANES, CHUNK), 0) == z

    def potential(n, half):
        if n == NSTEPS - 1:
            return ulast[half]
        return entry[n + 1, half, HALO : HALO + BX, VTOP : VTOP + BY]

    def gather(n):
        for half in range(2):
            rows = potential(n, half).reshape(ROWS, LANES).T
            high = rows.astype(BF16)
            ut[half * LANES : (half + 1) * LANES, :] = high
            ut[(2 + half) * LANES : (3 + half) * LANES, :] = (rows - high.astype(F32)).astype(BF16)

        def at(k, carry):
            found = []
            for sign in range(2):
                hot, depth = locate(sign, k)
                both = jnp.dot(ut[...], hot, preferred_element_type=F32)
                value = both[: 2 * LANES] + both[2 * LANES :]
                found.append(jnp.sum(jnp.where(depth, value, 0.0), axis=0, keepdims=True))
            part[n, :, pl.ds(pl.multiple_of(k * CHUNK, CHUNK), CHUNK)] = found[0] - found[1]
            return carry

        lax.fori_loop(0, NDIP // CHUNK, at, 0)

    def scatter(n):
        acc[n - 1] = jnp.zeros((ROWS, 4 * LANES), F32)

        def at(k, carry):
            value = res[n, :, pl.ds(pl.multiple_of(k * CHUNK, CHUNK), CHUNK)]
            for sign in range(2):
                hot, depth = locate(sign, k)
                placed = jnp.where(depth, value if sign == 0 else -value, 0.0)
                high = placed.astype(BF16)
                low = (placed - high.astype(F32)).astype(BF16)
                acc[n - 1] += lax.dot_general(
                    hot, jnp.concatenate([high, low], axis=0), (((1,), (1,)), ((), ())), preferred_element_type=F32
                )
            return carry

        lax.fori_loop(0, NDIP // CHUNK, at, 0)

    def injected(n, half, x):
        rows = pl.ds(pl.multiple_of(x * BY, BY), BY)
        return (
            acc[n - 1, rows, half * LANES : (half + 1) * LANES]
            + acc[n - 1, rows, (2 + half) * LANES : (3 + half) * LANES]
        )

    take_field(U0)
    halo_start(entry.at[0], VTOP, 0)
    take_field(R0)
    halo_start(rhs.at[0], HALO, 5)
    take_static(COND)

    def inverse(x):
        for half in range(2):
            inv[half, HALO + x, HALO : HALO + BY] = 1.0 / (6.0 + sblk[COND, half, x])

    over_x(inverse)
    halo_start(inv, HALO, 8)
    pieces(later_fields)
    send_static(CHG)
    send_static(RLX)
    send_field(R1)
    halo_wait(entry.at[0], VTOP, 0)
    halo_wait(rhs.at[0], HALO, 5)
    halo_wait(inv, HALO, 8)

    def statics(x):
        for half in range(2):
            c, g = sblk[COND, half, x], sblk[CHG, half, x]
            rate = 1.0 / sblk[RLX, half, x]
            a0, a1, b0, b1 = (jnp.zeros((BY, LANES), F32) for _ in range(4))
            for k in range(4):
                decay = jnp.exp(-rate / RATIOS[k])
                fresh = WEIGHTS[k] * (1.0 - decay)
                a0 = a0 + fresh
                a1 = a1 + fresh * decay
                tilt = decay * (WEIGHTS[k] / RATIOS[k])
                b0 = b0 + tilt
                b1 = b1 + tilt * (1.0 - 2.0 * decay)
            f1[half, x] = c * g * a0
            f2[half, x] = c * g * a1
            ka0[half, x] = c * a0
            ka1[half, x] = c * a1
            kb0[half, x] = c * g * rate * rate * b0
            kb1[half, x] = c * g * rate * rate * b1

    def block_of(k, half, x):
        return entry[k, half, HALO + x, VTOP : VTOP + BY]

    def forward(n):
        def body(half, x, total):
            return (rhs[n, half, x] + total) * inv[half, x]

        def closing(x, sums):
            for half in range(2):
                made = (rhs[n, half, x, HALO : HALO + BY] + sums[half]) * inv[half, x, HALO : HALO + BY]
                if n == NSTEPS - 1:
                    ulast[half, x - HALO] = made
                else:
                    entry[n + 1, half, x, VTOP : VTOP + BY] = made

        sweeps(entry.at[n], JACOBI, body, closing)

    forward(0)
    halo_start(entry.at[1], VTOP, 1)
    take_static(CHG)
    take_static(RLX)
    over_x(statics)
    take_field(R1)

    def step_one(x):
        for half in range(2):
            rhs[1, half, HALO + x, HALO : HALO + BY] = blk[R1, half, x] + f1[half, x] * block_of(1, half, x)

    over_x(step_one)
    halo_start(rhs.at[1], HALO, 6)
    send_field(R2)
    obs_pair_in.wait_recv()
    over(SLOTS, lambda p: obs_copy(p, 0).start(), 1)
    over(SLOTS, lambda p: obs_copy(p, 1).start(), 1)
    gather(0)
    halo_wait(entry.at[1], VTOP, 1)
    halo_wait(rhs.at[1], HALO, 6)
    forward(1)
    halo_start(entry.at[2], VTOP, 2)
    take_field(R2)

    def step_two(x):
        for half in range(2):
            rhs[2, half, HALO + x, HALO : HALO + BY] = (
                blk[R2, half, x] + f2[half, x] * block_of(1, half, x) + f1[half, x] * block_of(2, half, x)
            )

    over_x(step_two)
    halo_start(rhs.at[2], HALO, 7)
    send_field(T1)
    send_field(T2)
    over(SLOTS, lambda p: obs_wait(p, 0), 1)
    over(SLOTS, lambda p: obs_wait(p, 1), 1)
    obs_rows(True).start()
    gather(1)
    halo_wait(entry.at[2], VTOP, 2)
    halo_wait(rhs.at[2], HALO, 7)
    forward(2)
    gather(2)
    obs_rows(False).wait_recv()

    def row_copy(p):
        to = lax.rem(gx + p, NXB)
        return remote(part, prx.at[gx], psend.at[0, to], precv.at[0, gx], {"space": device(bx, to, mine)})

    def row_wait(p):
        of = lax.rem(gx + p, NXB)
        remote(part, prx.at[of], psend.at[0, of], precv.at[0, of], {"space": device(bx, of, mine)}).wait_recv()

    over(4, lambda p: row_copy(p).start(), 1)
    prx[gx] = part[...]
    over(4, row_wait, 1)
    res[...] = (prx[0] + prx[1]) + (prx[2] + prx[3])

    def col_copy(p):
        to = lax.rem(bx + p, NB)
        return remote(res, pry.at[bx], psend.at[1, to], precv.at[1, bx], {"space": device(to, gx, mine)})

    def col_wait(p):
        of = lax.rem(bx + p, NB)
        remote(res, pry.at[of], psend.at[1, of], precv.at[1, of], {"space": device(of, gx, mine)}).wait_recv()

    over(4, lambda p: col_copy(p).start(), 1)
    pry[bx] = res[...]
    over(4, col_wait, 1)
    over(4, lambda p: col_copy(p).wait_send(), 1)
    squares = jnp.zeros((1, NDIP), F32)
    for n in range(NSTEPS):
        volts = live[...] * ((pry[0, n] + pry[1, n]) + (pry[2, n] + pry[3, n]))
        part_resid = live[...] * (volts - obs_all[n])
        pry[0, n] = volts
        res[n] = part_resid
        squares = squares + part_resid * part_resid

    own = pl.ds(pl.multiple_of(space * LANES, LANES), LANES)
    other = pl.ds(pl.multiple_of(partner * LANES, LANES), LANES)
    swap = remote(pry.at[0, :, :, other], vswap.at[pl.ds(6, 3)], qsend.at[2], qrecv.at[2], {"space": partner})
    swap.start()
    lanes = squares[:, 0:LANES]
    for j in range(1, NDIP // LANES):
        lanes = lanes + squares[:, j * LANES : (j + 1) * LANES]
    sq[...] = lanes
    pair = remote(sq, sqc, qsend.at[3], qrecv.at[3], {"space": partner})
    pair.start()
    for n in range(NSTEPS):
        volts_out[n, pl.ds(mine, 1), :] = pry[0, n, :, own]
    swap.wait()
    for n in range(NSTEPS):
        volts_out[n, pl.ds(1 - mine, 1), :] = vswap[6 + n]
    pair.wait()
    sqz[tx] = sq[...] + sqc[...]

    def sq_copy(p):
        to = lax.rem(tx + p, 4)
        return remote(sqz.at[tx], sqz.at[tx], tsend.at[2, to], trecv.at[2, tx], {"tx": to})

    def sq_wait(p):
        of = lax.rem(tx + p, 4)
        remote(sqz.at[of], sqz.at[of], tsend.at[2, of], trecv.at[2, of], {"tx": of}).wait_recv()

    over(4, lambda p: sq_copy(p).start(), 1)

    def begin_adjoint(n):
        def body(x):
            for half in range(2):
                field = injected(n, half, x)
                if n == 1:
                    field = field + back[half, x] + f1[half, x] * adj[1, half, HALO + x, HALO : HALO + BY]
                scaled = field * inv[half, HALO + x, HALO : HALO + BY]
                adj[n - 1, half, HALO + x, HALO : HALO + BY] = scaled
                entry[5 - n, half, HALO + x, VTOP : VTOP + BY] = scaled

        over_x(body)

    def adjoint(n):
        def body(half, x, total):
            scaled = total * inv[half, x]
            adj[n - 1, half, x] += scaled
            return scaled

        def closing(x, sums):
            for half in range(2):
                back[half, x - HALO] = sums[half]

        sweeps(entry.at[5 - n], JACOBI if n == 2 else JACOBI - 1, body, closing)

    scatter(2)
    begin_adjoint(2)
    halo_start(entry.at[3], VTOP, 3)
    scatter(1)
    halo_wait(entry.at[3], VTOP, 3)
    adjoint(2)
    begin_adjoint(1)
    halo_start(entry.at[4], VTOP, 4)
    halo_wait(entry.at[4], VTOP, 4)
    adjoint(1)

    take_field(T1)
    take_field(T2)

    def gradients(x):
        for half in range(2):
            s1, s2 = (adj[k, half, HALO + x, HALO : HALO + BY] for k in range(2))
            u0, u1 = block_of(1, half, x), block_of(2, half, x)
            same = s2 * u1 + s1 * u0
            cross = s2 * u0
            grad[0, x // 2, half, lax.rem(x, 2)] = ka0[half, x] * same + ka1[half, x] * cross
            grad[1, x // 2, half, lax.rem(x, 2)] = (
                s1 * blk[T1, half, x] + s2 * blk[T2, half, x] - kb0[half, x] * same + kb1[half, x] * cross
            )

    over_x(gradients)

    def back_copy(f, p):
        j = lax.rem(p + slot, SLOTS)
        to = bx * SLOTS + j
        return to, remote(grad.at[f, j], rx.at[f, gx, mine], gsend.at[f, j], grecv.at[f, 2 * gx + mine], {"space": to})

    def back_wait(f, q):
        of = device(yp, q // 2, lax.rem(q, 2))
        here = rx.at[f, q // 2, lax.rem(q, 2)]
        copy = remote(here, here, gsend.at[f, q], grecv.at[f, q], {"space": of})
        pl.when(of != space)(copy.wait_recv)

    def tx_copy(f, p):
        to = lax.rem(tx + p, 4)
        return remote(rsum.at[f, to], rz.at[f, tx], tsend.at[f, to], trecv.at[f, tx], {"tx": to})

    def tx_wait(f, p):
        of = lax.rem(tx + p, 4)
        remote(rsum.at[f, of], rz.at[f, of], tsend.at[f, of], trecv.at[f, of], {"tx": of}).wait_recv()

    for f in range(2):
        begin(f, back_copy)

        def keep(f=f):
            rx[f, gx, mine] = grad[f, slot]

        pl.when(bx == yp)(keep)
    over(4, sq_wait, 1)
    total = (sqz[0] + sqz[1]) + (sqz[2] + sqz[3])
    misfit = jnp.sqrt(1.0 + jnp.sum(total, axis=1, keepdims=True))
    misfit_out[...] = misfit
    scale = 1.0 / misfit
    for f in range(2):
        over(SLOTS, functools.partial(back_wait, f))
        for row in range(4):
            rsum[f, row] = rx[f, row, 0] + rx[f, row, 1]
        over(4, lambda p: tx_copy(f, p).start(), 1)
        rz[f, tx] = rsum[f, tx]
    for f, out in ((0, gc_out), (1, gt_out)):
        over(4, functools.partial(tx_wait, f), 1)
        for half in range(2):
            value = (rz[f, 0, half] + rz[f, 1, half]) + (rz[f, 2, half] + rz[f, 3, half])
            out[:, :, half * LANES : (half + 1) * LANES] = value * scale.reshape(1, 1, 1)

    for f in range(6):
        finish(f, field_copy)
    for f in range(3):
        finish(f, static_copy)
    obs_pair.wait_send()
    for which in range(2):
        over(SLOTS, lambda p: obs_copy(p, which).wait_send(), 1)
    obs_rows(True).wait_send()
    over(4, lambda p: row_copy(p).wait_send(), 1)
    over(4, lambda p: sq_copy(p).wait_send(), 1)
    for f in range(2):
        finish(f, back_copy)
        over(4, lambda p: tx_copy(f, p).wait_send(), 1)


def on_device(cond, chg, rlx, start, mem, src_cells, dip, counts, obs):
    vmem = pl.BlockSpec(memory_space=pltpu.VMEM)
    smem = pl.BlockSpec(memory_space=pltpu.SMEM)
    field = pltpu.VMEM((2, BX, BY, LANES), F32)
    dma = pltpu.SemaphoreType.DMA
    wide = pltpu.VMEM((2, EX, EY + 2 * PAD, LANES), F32)
    scratch = [
        pltpu.VMEM((6, 2, NXB, 2, 2, BY, LANES), F32),
        pltpu.VMEM((3, NXB, 2, 2, BY, LANES), F32),
        pltpu.VMEM((4, 2, BX, BY, LANES), F32),
        pltpu.VMEM((3, 2, BX, BY, LANES), F32),
        pltpu.VMEM((5, 2, EX, EY + 2 * PAD, LANES), F32),
        wide, wide,
        pltpu.VMEM((2, EX, EY, LANES), F32),
        pltpu.VMEM((NSTEPS, 2, EX, EY, LANES), F32),
        field, field, field, field, field, field,
        field,
        pltpu.VMEM((2, 2, EX, EY, LANES), F32),
        field,
        pltpu.VMEM((4 * LANES, ROWS), BF16),
        pltpu.VMEM((2, ROWS, 4 * LANES), F32),
        pltpu.VMEM((NSTEPS, 1, NDIP), F32),
        pltpu.VMEM((NXB, NSTEPS, 1, NDIP), F32),
        pltpu.VMEM((NB, NSTEPS, 1, NDIP), F32),
        pltpu.VMEM((NSTEPS, 1, NDIP), F32),
        pltpu.VMEM((NSTEPS, 1, NDIP), F32),
        pltpu.VMEM((1, NDIP), F32),
        pltpu.VMEM((9, 1, LANES), F32),
        pltpu.VMEM((1, LANES), F32),
        pltpu.VMEM((1, LANES), F32),
        pltpu.VMEM((4, 1, LANES), F32),
        pltpu.VMEM((2, SLOTS, 2, 2, BY, LANES), F32),
        pltpu.VMEM((2, NXB, 2, 2, 2, BY, LANES), F32),
        pltpu.VMEM((2, NXB, 2, 2, BY, LANES), F32),
        pltpu.VMEM((2, 4, 2, 2, BY, LANES), F32),
        dma((6, SLOTS)), dma((6, SLOTS)), dma((3, SLOTS)), dma((3, SLOTS)),
        dma((9, 8)), dma((9, 8)),
        dma((2, SLOTS)), dma((2, SLOTS)),
        dma((2, 4)), dma((2, 4)),
        dma((4,)), dma((4,)),
        dma((2, SLOTS)), dma((2, SLOTS)),
        dma((3, 4)), dma((3, 4)),
    ]
    volts, misfit, grad_c, grad_t = pl.pallas_call(
        kernel,
        out_shape=(
            jax.ShapeDtypeStruct((NSTEPS, 2, LANES), F32),
            jax.ShapeDtypeStruct((1, 1), F32),
            jax.ShapeDtypeStruct((2, BY, 2 * LANES), F32),
            jax.ShapeDtypeStruct((2, BY, 2 * LANES), F32),
        ),
        in_specs=[vmem, vmem, vmem, vmem, vmem, smem, vmem, smem, vmem],
        out_specs=(vmem, vmem, vmem, vmem),
        scratch_shapes=scratch,
        compiler_params=pltpu.CompilerParams(has_side_effects=True, vmem_limit_bytes=60 << 20),
    )(cond, chg, rlx, start, mem, src_cells, dip, counts, obs)
    return (volts, misfit.reshape(()), grad_c, grad_t)


def solution(mesh):
    placed = (
        P("space", None, None),
        P("space", None, None),
        P("space", None, None),
        P("tx", "space", None, None),
        P(None, "tx", "space", None, None),
        P(None, "tx"),
        P(),
        P(),
        P(None, "tx", "space"),
    )
    return jax.shard_map(
        on_device,
        mesh=mesh,
        in_specs=placed,
        out_specs=(P(None, "tx", "space"), P(), P("space", "tx", None), P("space", "tx", None)),
        check_vma=False,
    )
```

time: 312 us -> 201 us (0.64)
  Pallas kernels: 302 us -> 194 us
    pallas_call x1, Pallas kernels: 302 us -> 194 us  [on_device(): pl.pallas_call(kernel, out_shape=(jax.ShapeDtypeStruct((NSTEPS, 2, LANES)...]
where the time goes in v2:
time: 201 us; the launch traced here: 200 us
  Pallas kernels  194 us (97%)
  local copies, waits for them, and re-layouts  4.21 us (2%)
  between operations  2.4 us (1%)
    pallas_call x1, Pallas kernels, on_device(): pl.pallas_call(kernel, out_shape=(jax.ShapeDtypeStruct((NSTEPS, 2, LANES)...  194 us
    unnamed x3, local copies, waits for them, and re-layouts  4.21 us

profile of v2, /device:TPU:19, one launch (start us, length us, event | category | flops | bytes accessed | tf_op | source)
XLA Modules:
  0.0 200.4 jit_solution(10504863486880202520)
XLA Ops:
  0.6 193.8 %shard_map.120 = (f32[3,2,128]{2,1,0:T(2,128)}, f32[1,1]{1,0:T(1,128)}, f32[2,32,256]{2,1,0:T(8,128)}, f32[2,32,256]{2,1,0:T(8,128)}) custom-call(f32[2,128,256]{2,1,0:T(8,128)} %cond.1, f32[2,128,256]{2,1,0:T(8,128)} %chg.1, f32[2,128,256]{2,1,0:T(8,128)} %rlx.1, f32[2,2,128,256]{3,2,1,0:T(8,128)} %start.1, f32[4,2,2,128,256]{4,3,2,1,0:T(8,128)} %mem.1, ...), custom_call_target="tpu_custom_call" | custom-call | tf_op jit(solution)/shard_map/pallas_call | solution.py:707
  194.4 1.3 copy.17
  196.3 1.5 copy.19
  197.8 1.5 copy.20

commit v3 on v2

--- a/solution.py
+++ b/solution.py
@@ -27,9 +27,11 @@
 CHUNK = 512
 ROWS = BX * BY
 UNROLL = 4
-R1, R2, T1, T2 = range(4)
-COND, CHG, RLX = range(3)
-U0, R0 = 4, 5
+U0, R0, R1, R2 = range(4)
+COND, F1, F2 = range(3)
+KA0, KA1, KB0, KB1 = range(4)
+POT0, POT1, DUAL2, DUAL1 = range(4)
+SPACES = 32
 SIDES = tuple((i, j) for i in (-1, 0, 1) for j in (-1, 0, 1) if (i, j) != (0, 0))
 
 
@@ -40,13 +42,15 @@
 
 
 def kernel(
-    cond, chg, rlx, start, mem, src_cells, dip, counts, obs,
+    cond_hbm, chg_hbm, rlx_hbm, start_hbm, mem_hbm, src_cells, dip, counts, obs,
     volts_out, misfit_out, gc_out, gt_out,
-    stage, sstage, blk, sblk, entry, va, vb,
-    inv, rhs, f1, f2, ka0, ka1, kb0, kb1, ulast, adj, back,
+    cond, chg, rlx, start, mem,
+    stage, sstage, tilts, factors, blk, sblk, entry, va, vb,
+    inv, rhs, ulast, adj, back,
     ut, acc, part, prx, pry, res, obs_all, live, vswap, sq, sqc, sqz,
-    grad, rx, rsum, rz,
-    fsend, frecv, ssend, srecv, hsend, hrecv, osend, orecv, psend, precv, qsend, qrecv, gsend, grecv, tsend, trecv,
+    rx, rsum, rz,
+    lsem, fsend, frecv, ssend, srecv, zsend, zrecv, hsend, hrecv, osend, orecv, psend, precv, qsend, qrecv,
+    gsend, grecv, tsend, trecv,
 ):
     space = lax.axis_index("space")
     tx = lax.axis_index("tx")
@@ -66,6 +70,25 @@
             return carry
 
         lax.fori_loop(first, count, at, 0)
+
+    barrier = pltpu.get_barrier_semaphore()
+    loads = [
+        pltpu.make_async_copy(a, b, lsem.at[i])
+        for i, (a, b) in enumerate(
+            ((cond_hbm, cond), (start_hbm, start), (mem_hbm, mem), (chg_hbm, chg), (rlx_hbm, rlx))
+        )
+    ]
+    for load in loads:
+        load.start()
+
+    def greet_space(q):
+        pl.semaphore_signal(barrier, 1, device_id={"space": lax.rem(space + q, SPACES)}, device_id_type=MESH)
+
+    def greet_tx(q):
+        pl.semaphore_signal(barrier, 1, device_id={"tx": lax.rem(tx + q, 4)}, device_id_type=MESH)
+
+    over(SPACES, greet_space, 1)
+    over(4, greet_tx, 1)
 
     def pieces(body):
         def at(i, carry):
@@ -89,12 +112,23 @@
             stage[R0, t, row, half, layer] = source + c * total
 
     def later_fields(row, layer, half, where):
-        c = cond[where]
-        relax = rlx[where]
-        sstage[CHG, row, half, layer] = chg[where]
-        sstage[RLX, row, half, layer] = relax
-        rate = 1.0 / relax
+        c, g = cond[where], chg[where]
+        rate = 1.0 / rlx[where]
         decays = [jnp.exp(-rate / ratio) for ratio in RATIOS]
+        a0, a1, b0, b1 = (jnp.zeros((BY, LANES), F32) for _ in range(4))
+        for k in range(4):
+            fresh = WEIGHTS[k] * (1.0 - decays[k])
+            a0 = a0 + fresh
+            a1 = a1 + fresh * decays[k]
+            tilt = decays[k] * (WEIGHTS[k] / RATIOS[k])
+            b0 = b0 + tilt
+            b1 = b1 + tilt * (1.0 - 2.0 * decays[k])
+        sstage[F1, row, half, layer] = c * g * a0
+        sstage[F2, row, half, layer] = c * g * a1
+        factors[KA0, row, half, layer] = c * a0
+        factors[KA1, row, half, layer] = c * a1
+        factors[KB0, row, half, layer] = c * g * rate * rate * b0
+        factors[KB1, row, half, layer] = c * g * rate * rate * b1
         for t in range(2):
             first, second, slope, slope_d = (jnp.zeros((BY, LANES), F32) for _ in range(4))
             for k in range(4):
@@ -106,8 +140,8 @@
                 slope_d = slope_d + decays[k] * tilt
             stage[R1, t, row, half, layer] = c * first
             stage[R2, t, row, half, layer] = c * second
-            stage[T1, t, row, half, layer] = c * rate * rate * slope
-            stage[T2, t, row, half, layer] = 2.0 * c * rate * rate * slope_d
+            tilts[0, t, row, half, layer] = c * rate * rate * slope
+            tilts[1, t, row, half, layer] = 2.0 * c * rate * rate * slope_d
 
     def landing(f, j):
         layers = pl.ds(HALO + 2 * j, 2)
@@ -115,7 +149,7 @@
             return entry.at[0, :, layers, pl.ds(VTOP, BY)]
         if f == R0:
             return rhs.at[0, :, layers, pl.ds(HALO, BY)]
-        return blk.at[f, :, pl.ds(2 * j, 2)]
+        return blk.at[f - R1, :, pl.ds(2 * j, 2)]
 
     def target(p):
         q = lax.rem(p + slot, SLOTS)
@@ -127,7 +161,10 @@
 
     def static_copy(f, p):
         x, t, q, to = target(p)
-        return to, remote(sstage.at[f, x], sblk.at[f, :, pl.ds(2 * slot, 2)], ssend.at[f, q], srecv.at[f, slot], {"space": to})
+        quarter = (tx // 2, lax.rem(tx, 2))
+        return to, remote(
+            sstage.at[(f, x) + quarter], sblk.at[(f,) + quarter + (slot,)], ssend.at[f, q], srecv.at[f, slot], {"space": to}
+        )
 
     def begin(f, copy_of):
         def one(p):
@@ -152,7 +189,7 @@
             elif f == R0:
                 rhs[0, :, pl.ds(HALO + 2 * slot, 2), HALO : HALO + BY] = stage[f, mine, gx]
             else:
-                blk[f, :, pl.ds(2 * slot, 2)] = stage[f, mine, gx]
+                blk[f - R1, :, pl.ds(2 * slot, 2)] = stage[f, mine, gx]
 
         pl.when(bx == yp)(keep)
 
@@ -160,7 +197,7 @@
         begin(f, static_copy)
 
         def keep():
-            sblk[f, :, pl.ds(2 * slot, 2)] = sstage[f, gx]
+            sblk[f, tx // 2, lax.rem(tx, 2), slot] = sstage[f, gx, tx // 2, lax.rem(tx, 2)]
 
         pl.when(bx == yp)(keep)
 
@@ -173,19 +210,35 @@
 
         over(SLOTS, one)
 
-    def take_static(f):
+    def spread_copy(f, p):
+        to = lax.rem(tx + p, 4)
+        quarter = sblk.at[f, tx // 2, lax.rem(tx, 2)]
+        return remote(quarter, quarter, zsend.at[f, to], zrecv.at[f, tx], {"tx": to})
+
+    def spread_static(f):
         def one(j):
-            here = sblk.at[f, :, pl.ds(2 * j, 2)]
+            here = sblk.at[f, tx // 2, lax.rem(tx, 2), j]
             of = bx * SLOTS + j
             copy = remote(here, here, ssend.at[f, j], srecv.at[f, j], {"space": of})
             pl.when(of != space)(copy.wait_recv)
 
         over(SLOTS, one)
-
+        over(4, lambda p: spread_copy(f, p).start(), 1)
+
+    def take_static(f):
+        def one(p):
+            of = lax.rem(tx + p, 4)
+            quarter = sblk.at[f, of // 2, lax.rem(of, 2)]
+            remote(quarter, quarter, zsend.at[f, of], zrecv.at[f, of], {"tx": of}).wait_recv()
+
+        over(4, one, 1)
+
+    def static(f, half, x):
+        return sblk[f, half, lax.rem(x, 2), x // 2]
+
+    for load in loads[:3]:
+        load.wait()
     pieces(first_fields)
-    send_field(U0)
-    send_field(R0)
-    send_static(COND)
 
     def clear(ref, index):
         shape = ref.at[index].shape
@@ -231,6 +284,11 @@
     pl.when(gx == NXB - 1)(lambda: clear_rows(False))
     pl.when(bx == 0)(lambda: clear_layers(True))
     pl.when(bx == NB - 1)(lambda: clear_layers(False))
+
+    pl.semaphore_wait(barrier, SPACES + 2)
+    send_static(COND)
+    send_field(U0)
+    send_field(R0)
 
     def slab_lanes(s, count=1):
         return pl.ds(pl.multiple_of(s * LANES, LANES), count * LANES)
@@ -272,9 +330,11 @@
     lax.fori_loop(0, NB * SLOTS, live_at, 0)
 
     def halo(ref, top, which):
+        width = HALO if top == VTOP else HALO - 1
         copies = []
         for side, (i, j) in enumerate(SIDES):
-            layers = {-1: (HALO, HALO, HALO + BX), 1: (BX, HALO, 0), 0: (HALO, BX, HALO)}[i]
+            deep = width if j == 0 else width - 1
+            layers = {-1: (HALO, deep, HALO + BX), 1: (HALO + BX - deep, deep, HALO - deep), 0: (HALO, BX, HALO)}[i]
             rows = {-1: (top, HALO, top + BY), 1: (top + BY - HALO, HALO, top - HALO), 0: (top, BY, top)}[j]
             sends = (bx + i >= 0) & (bx + i < NB) & (gx + j >= 0) & (gx + j < NXB)
             takes = (bx - i >= 0) & (bx - i < NB) & (gx - j >= 0) & (gx - j < NXB)
@@ -390,45 +450,30 @@
             + acc[n - 1, rows, (2 + half) * LANES : (3 + half) * LANES]
         )
 
+    spread_static(COND)
+    for load in loads[3:]:
+        load.wait()
+    pieces(later_fields)
     take_field(U0)
     halo_start(entry.at[0], VTOP, 0)
+    take_static(COND)
+
+    def inverse(x):
+        for half in range(2):
+            inv[half, HALO + x, HALO : HALO + BY] = 1.0 / (6.0 + static(COND, half, x))
+
+    over_x(inverse)
+    halo_start(inv, HALO, 8)
     take_field(R0)
     halo_start(rhs.at[0], HALO, 5)
-    take_static(COND)
-
-    def inverse(x):
-        for half in range(2):
-            inv[half, HALO + x, HALO : HALO + BY] = 1.0 / (6.0 + sblk[COND, half, x])
-
-    over_x(inverse)
-    halo_start(inv, HALO, 8)
-    pieces(later_fields)
-    send_static(CHG)
-    send_static(RLX)
+    send_static(F1)
+    send_static(F2)
+    halo_wait(entry.at[0], VTOP, 0)
+    halo_wait(inv, HALO, 8)
+    halo_wait(rhs.at[0], HALO, 5)
     send_field(R1)
-    halo_wait(entry.at[0], VTOP, 0)
-    halo_wait(rhs.at[0], HALO, 5)
-    halo_wait(inv, HALO, 8)
-
-    def statics(x):
-        for half in range(2):
-            c, g = sblk[COND, half, x], sblk[CHG, half, x]
-            rate = 1.0 / sblk[RLX, half, x]
-            a0, a1, b0, b1 = (jnp.zeros((BY, LANES), F32) for _ in range(4))
-            for k in range(4):
-                decay = jnp.exp(-rate / RATIOS[k])
-                fresh = WEIGHTS[k] * (1.0 - decay)
-                a0 = a0 + fresh
-                a1 = a1 + fresh * decay
-                tilt = decay * (WEIGHTS[k] / RATIOS[k])
-                b0 = b0 + tilt
-                b1 = b1 + tilt * (1.0 - 2.0 * decay)
-            f1[half, x] = c * g * a0
-            f2[half, x] = c * g * a1
-            ka0[half, x] = c * a0
-            ka1[half, x] = c * a1
-            kb0[half, x] = c * g * rate * rate * b0
-            kb1[half, x] = c * g * rate * rate * b1
+    spread_static(F1)
+    spread_static(F2)
 
     def block_of(k, half, x):
         return entry[k, half, HALO + x, VTOP : VTOP + BY]
@@ -449,38 +494,39 @@
 
     forward(0)
     halo_start(entry.at[1], VTOP, 1)
-    take_static(CHG)
-    take_static(RLX)
-    over_x(statics)
+    take_static(F1)
     take_field(R1)
 
     def step_one(x):
         for half in range(2):
-            rhs[1, half, HALO + x, HALO : HALO + BY] = blk[R1, half, x] + f1[half, x] * block_of(1, half, x)
+            rhs[1, half, HALO + x, HALO : HALO + BY] = (
+                blk[0, half, x] + static(F1, half, x) * block_of(1, half, x)
+            )
 
     over_x(step_one)
     halo_start(rhs.at[1], HALO, 6)
-    send_field(R2)
     obs_pair_in.wait_recv()
     over(SLOTS, lambda p: obs_copy(p, 0).start(), 1)
     over(SLOTS, lambda p: obs_copy(p, 1).start(), 1)
     gather(0)
     halo_wait(entry.at[1], VTOP, 1)
     halo_wait(rhs.at[1], HALO, 6)
+    send_field(R2)
     forward(1)
     halo_start(entry.at[2], VTOP, 2)
+    take_static(F2)
     take_field(R2)
 
     def step_two(x):
         for half in range(2):
             rhs[2, half, HALO + x, HALO : HALO + BY] = (
-                blk[R2, half, x] + f2[half, x] * block_of(1, half, x) + f1[half, x] * block_of(2, half, x)
+                blk[1, half, x]
+                + static(F2, half, x) * block_of(1, half, x)
+                + static(F1, half, x) * block_of(2, half, x)
             )
 
     over_x(step_two)
     halo_start(rhs.at[2], HALO, 7)
-    send_field(T1)
-    send_field(T2)
     over(SLOTS, lambda p: obs_wait(p, 0), 1)
     over(SLOTS, lambda p: obs_wait(p, 1), 1)
     obs_rows(True).start()
@@ -488,6 +534,38 @@
     halo_wait(entry.at[2], VTOP, 2)
     halo_wait(rhs.at[2], HALO, 7)
     forward(2)
+
+    def back_copy(f, p):
+        j = lax.rem(p + slot, SLOTS)
+        layers = pl.ds(HALO + 2 * j, 2)
+        if f in (POT0, POT1):
+            here = entry.at[f + 1, :, layers, pl.ds(VTOP, BY)]
+        else:
+            here = adj.at[DUAL1 - f, :, layers, pl.ds(HALO, BY)]
+        to = bx * SLOTS + j
+        return to, remote(here, rx.at[f, gx, mine], gsend.at[f, j], grecv.at[f, 2 * gx + mine], {"space": to})
+
+    def send_back(f):
+        begin(f, back_copy)
+
+        def keep():
+            layers = pl.ds(HALO + 2 * slot, 2)
+            if f in (POT0, POT1):
+                rx[f, gx, mine] = entry[f + 1, :, layers, VTOP : VTOP + BY]
+            else:
+                rx[f, gx, mine] = adj[DUAL1 - f, :, layers, HALO : HALO + BY]
+
+        pl.when(bx == yp)(keep)
+
+    def back_wait(f, q):
+        x, t = q // 2, lax.rem(q, 2)
+        of = device(yp, x, t)
+        here = rx.at[f, x, t]
+        copy = remote(here, here, gsend.at[f, q], grecv.at[f, q], {"space": of})
+        pl.when(of != space)(copy.wait_recv)
+
+    send_back(POT0)
+    send_back(POT1)
     gather(2)
     obs_rows(False).wait_recv()
 
@@ -557,7 +635,7 @@
             for half in range(2):
                 field = injected(n, half, x)
                 if n == 1:
-                    field = field + back[half, x] + f1[half, x] * adj[1, half, HALO + x, HALO : HALO + BY]
+                    field = field + back[half, x] + static(F1, half, x) * adj[1, half, HALO + x, HALO : HALO + BY]
                 scaled = field * inv[half, HALO + x, HALO : HALO + BY]
                 adj[n - 1, half, HALO + x, HALO : HALO + BY] = scaled
                 entry[5 - n, half, HALO + x, VTOP : VTOP + BY] = scaled
@@ -585,98 +663,99 @@
     begin_adjoint(1)
     halo_start(entry.at[4], VTOP, 4)
     halo_wait(entry.at[4], VTOP, 4)
+    send_back(DUAL2)
     adjoint(1)
-
-    take_field(T1)
-    take_field(T2)
-
-    def gradients(x):
-        for half in range(2):
-            s1, s2 = (adj[k, half, HALO + x, HALO : HALO + BY] for k in range(2))
-            u0, u1 = block_of(1, half, x), block_of(2, half, x)
-            same = s2 * u1 + s1 * u0
-            cross = s2 * u0
-            grad[0, x // 2, half, lax.rem(x, 2)] = ka0[half, x] * same + ka1[half, x] * cross
-            grad[1, x // 2, half, lax.rem(x, 2)] = (
-                s1 * blk[T1, half, x] + s2 * blk[T2, half, x] - kb0[half, x] * same + kb1[half, x] * cross
-            )
-
-    over_x(gradients)
-
-    def back_copy(f, p):
-        j = lax.rem(p + slot, SLOTS)
-        to = bx * SLOTS + j
-        return to, remote(grad.at[f, j], rx.at[f, gx, mine], gsend.at[f, j], grecv.at[f, 2 * gx + mine], {"space": to})
-
-    def back_wait(f, q):
-        of = device(yp, q // 2, lax.rem(q, 2))
-        here = rx.at[f, q // 2, lax.rem(q, 2)]
-        copy = remote(here, here, gsend.at[f, q], grecv.at[f, q], {"space": of})
-        pl.when(of != space)(copy.wait_recv)
-
-    def tx_copy(f, p):
-        to = lax.rem(tx + p, 4)
-        return remote(rsum.at[f, to], rz.at[f, tx], tsend.at[f, to], trecv.at[f, tx], {"tx": to})
-
-    def tx_wait(f, p):
-        of = lax.rem(tx + p, 4)
-        remote(rsum.at[f, of], rz.at[f, of], tsend.at[f, of], trecv.at[f, of], {"tx": of}).wait_recv()
-
-    for f in range(2):
-        begin(f, back_copy)
-
-        def keep(f=f):
-            rx[f, gx, mine] = grad[f, slot]
-
-        pl.when(bx == yp)(keep)
+    send_back(DUAL1)
+
     over(4, sq_wait, 1)
     total = (sqz[0] + sqz[1]) + (sqz[2] + sqz[3])
     misfit = jnp.sqrt(1.0 + jnp.sum(total, axis=1, keepdims=True))
     misfit_out[...] = misfit
     scale = 1.0 / misfit
-    for f in range(2):
+    for f in (POT0, POT1, DUAL2):
         over(SLOTS, functools.partial(back_wait, f))
-        for row in range(4):
-            rsum[f, row] = rx[f, row, 0] + rx[f, row, 1]
-        over(4, lambda p: tx_copy(f, p).start(), 1)
-        rz[f, tx] = rsum[f, tx]
+
+    def tx_copy(f, to):
+        return remote(rsum.at[f, to], rz.at[f, tx], tsend.at[f, to], trecv.at[f, tx], {"tx": to})
+
+    def tx_wait(f, p):
+        of = lax.rem(tx + p, 4)
+        remote(rsum.at[f, of], rz.at[f, of], tsend.at[f, of], trecv.at[f, of], {"tx": of}).wait_recv()
+
+    def gradients(i):
+        x = lax.rem(gx + i, NXB)
+        for t in range(2):
+            back_wait(DUAL1, 2 * x + t)
+        for half in range(2):
+            for layer in range(2):
+                at = (half, layer)
+                same, cross, tilt = (jnp.zeros((BY, LANES), F32) for _ in range(3))
+                for t in range(2):
+                    u0, u1, s2, s1 = (rx[(f, x, t) + at] for f in range(4))
+                    same = same + (s2 * u1 + s1 * u0)
+                    cross = cross + s2 * u0
+                    tilt = tilt + (s1 * tilts[(0, t, x) + at] + s2 * tilts[(1, t, x) + at])
+                ka0, ka1, kb0, kb1 = (factors[(f, x) + at] for f in range(4))
+                rsum[(0, x) + at] = ka0 * same + ka1 * cross
+                rsum[(1, x) + at] = tilt - kb0 * same + kb1 * cross
+
+        def give():
+            for f in range(2):
+                tx_copy(f, x).start()
+
+        def keep():
+            for f in range(2):
+                rz[f, tx] = rsum[f, x]
+
+        pl.when(x != tx)(give)
+        pl.when(x == tx)(keep)
+
+    over(NXB, gradients)
     for f, out in ((0, gc_out), (1, gt_out)):
         over(4, functools.partial(tx_wait, f), 1)
         for half in range(2):
             value = (rz[f, 0, half] + rz[f, 1, half]) + (rz[f, 2, half] + rz[f, 3, half])
             out[:, :, half * LANES : (half + 1) * LANES] = value * scale.reshape(1, 1, 1)
 
-    for f in range(6):
+    for f in range(4):
         finish(f, field_copy)
     for f in range(3):
         finish(f, static_copy)
+        over(4, lambda p: spread_copy(f, p).wait_send(), 1)
     obs_pair.wait_send()
     for which in range(2):
         over(SLOTS, lambda p: obs_copy(p, which).wait_send(), 1)
     obs_rows(True).wait_send()
     over(4, lambda p: row_copy(p).wait_send(), 1)
     over(4, lambda p: sq_copy(p).wait_send(), 1)
+    for f in range(4):
+        finish(f, back_copy)
     for f in range(2):
-        finish(f, back_copy)
-        over(4, lambda p: tx_copy(f, p).wait_send(), 1)
+        over(4, lambda p: tx_copy(f, lax.rem(tx + p, 4)).wait_send(), 1)
 
 
 def on_device(cond, chg, rlx, start, mem, src_cells, dip, counts, obs):
     vmem = pl.BlockSpec(memory_space=pltpu.VMEM)
+    whole = pl.BlockSpec(memory_space=pl.ANY)
     smem = pl.BlockSpec(memory_space=pltpu.SMEM)
     field = pltpu.VMEM((2, BX, BY, LANES), F32)
     dma = pltpu.SemaphoreType.DMA
     wide = pltpu.VMEM((2, EX, EY + 2 * PAD, LANES), F32)
+    slab = pltpu.VMEM((2, 128, 2 * LANES), F32)
     scratch = [
-        pltpu.VMEM((6, 2, NXB, 2, 2, BY, LANES), F32),
+        slab, slab, slab,
+        pltpu.VMEM((2, 2, 128, 2 * LANES), F32),
+        pltpu.VMEM((4, 2, 2, 128, 2 * LANES), F32),
+        pltpu.VMEM((4, 2, NXB, 2, 2, BY, LANES), F32),
         pltpu.VMEM((3, NXB, 2, 2, BY, LANES), F32),
-        pltpu.VMEM((4, 2, BX, BY, LANES), F32),
-        pltpu.VMEM((3, 2, BX, BY, LANES), F32),
+        pltpu.VMEM((2, 2, NXB, 2, 2, BY, LANES), F32),
+        pltpu.VMEM((4, NXB, 2, 2, BY, LANES), F32),
+        pltpu.VMEM((2, 2, BX, BY, LANES), F32),
+        pltpu.VMEM((3, 2, 2, BX // 2, BY, LANES), F32),
         pltpu.VMEM((5, 2, EX, EY + 2 * PAD, LANES), F32),
         wide, wide,
         pltpu.VMEM((2, EX, EY, LANES), F32),
         pltpu.VMEM((NSTEPS, 2, EX, EY, LANES), F32),
-        field, field, field, field, field, field,
         field,
         pltpu.VMEM((2, 2, EX, EY, LANES), F32),
         field,
@@ -692,16 +771,17 @@
         pltpu.VMEM((1, LANES), F32),
         pltpu.VMEM((1, LANES), F32),
         pltpu.VMEM((4, 1, LANES), F32),
-        pltpu.VMEM((2, SLOTS, 2, 2, BY, LANES), F32),
-        pltpu.VMEM((2, NXB, 2, 2, 2, BY, LANES), F32),
+        pltpu.VMEM((4, NXB, 2, 2, 2, BY, LANES), F32),
         pltpu.VMEM((2, NXB, 2, 2, BY, LANES), F32),
         pltpu.VMEM((2, 4, 2, 2, BY, LANES), F32),
-        dma((6, SLOTS)), dma((6, SLOTS)), dma((3, SLOTS)), dma((3, SLOTS)),
+        dma((5,)),
+        dma((4, SLOTS)), dma((4, SLOTS)), dma((3, SLOTS)), dma((3, SLOTS)),
+        dma((3, 4)), dma((3, 4)),
         dma((9, 8)), dma((9, 8)),
         dma((2, SLOTS)), dma((2, SLOTS)),
         dma((2, 4)), dma((2, 4)),
         dma((4,)), dma((4,)),
-        dma((2, SLOTS)), dma((2, SLOTS)),
+        dma((4, SLOTS)), dma((4, SLOTS)),
         dma((3, 4)), dma((3, 4)),
     ]
     volts, misfit, grad_c, grad_t = pl.pallas_call(
@@ -712,10 +792,10 @@
             jax.ShapeDtypeStruct((2, BY, 2 * LANES), F32),
             jax.ShapeDtypeStruct((2, BY, 2 * LANES), F32),
         ),
-        in_specs=[vmem, vmem, vmem, vmem, vmem, smem, vmem, smem, vmem],
+        in_specs=[whole, whole, whole, whole, whole, smem, vmem, smem, vmem],
         out_specs=(vmem, vmem, vmem, vmem),
         scratch_shapes=scratch,
-        compiler_params=pltpu.CompilerParams(has_side_effects=True, vmem_limit_bytes=60 << 20),
+        compiler_params=pltpu.CompilerParams(has_side_effects=True, collective_id=0, vmem_limit_bytes=60 << 20),
     )(cond, chg, rlx, start, mem, src_cells, dip, counts, obs)
     return (volts, misfit.reshape(()), grad_c, grad_t)
 

time: 201 us -> 176 us (0.88)
  Pallas kernels: 194 us -> 169 us
    pallas_call x1, Pallas kernels: 194 us -> 169 us  [on_device(): pl.pallas_call(kernel, out_shape=(jax.ShapeDtypeStruct((NSTEPS, 2, LANES)...]
where the time goes in v3:
time: 176 us; the launch traced here: 175 us
  Pallas kernels  169 us (96%)
  local copies, waits for them, and re-layouts  4.21 us (2%)
  between operations  2.4 us (1%)
    pallas_call x1, Pallas kernels, on_device(): pl.pallas_call(kernel, out_shape=(jax.ShapeDtypeStruct((NSTEPS, 2, LANES)...  169 us
    unnamed x3, local copies, waits for them, and re-layouts  4.21 us

profile of v3, /device:TPU:19, one launch (start us, length us, event | category | flops | bytes accessed | tf_op | source)
XLA Modules:
  0.0 175.5 jit_solution(2553256649687142785)
XLA Ops:
  0.6 168.9 %shard_map.120 = (f32[3,2,128]{2,1,0:T(2,128)}, f32[1,1]{1,0:T(1,128)}, f32[2,32,256]{2,1,0:T(8,128)}, f32[2,32,256]{2,1,0:T(8,128)}) custom-call(f32[2,128,256]{2,1,0:T(8,128)} %cond_hbm.1, f32[2,128,256]{2,1,0:T(8,128)} %chg_hbm.1, f32[2,128,256]{2,1,0:T(8,128)} %rlx_hbm.1, f32[2,2,128,256]{3,2,1,0:T(8,128)} %start_hbm.1, f32[4,2,2,128,256]{4,3,2,1,0:T(8,128)} %mem_hbm.1, ...), custom_call_target="tpu_custom_call" | custom-call | tf_op jit(solution)/shard_map/pallas_call | solution.py:787
  169.5 1.3 copy.17
  171.4 1.5 copy.19
  172.9 1.5 copy.20

commit v4 on v3

--- a/solution.py
+++ b/solution.py
@@ -26,7 +26,7 @@
 NDIP = 4096
 CHUNK = 512
 ROWS = BX * BY
-UNROLL = 4
+UNROLL = 8
 U0, R0, R1, R2 = range(4)
 COND, F1, F2 = range(3)
 KA0, KA1, KB0, KB1 = range(4)
@@ -45,7 +45,7 @@
     cond_hbm, chg_hbm, rlx_hbm, start_hbm, mem_hbm, src_cells, dip, counts, obs,
     volts_out, misfit_out, gc_out, gt_out,
     cond, chg, rlx, start, mem,
-    stage, sstage, tilts, factors, blk, sblk, entry, va, vb,
+    perm, hots, stage, sstage, tilts, factors, blk, sblk, entry, va, vb,
     inv, rhs, ulast, adj, back,
     ut, acc, part, prx, pry, res, obs_all, live, vswap, sq, sqc, sqz,
     rx, rsum, rz,
@@ -90,30 +90,62 @@
     over(SPACES, greet_space, 1)
     over(4, greet_tx, 1)
 
+    def three(value):
+        high = value.astype(BF16)
+        rest = value - high.astype(F32)
+        middle = rest.astype(BF16)
+        return high, middle, (rest - middle.astype(F32)).astype(BF16)
+
+    def reorder(value, axis):
+        parts = jnp.concatenate(three(value), axis=0)
+        moved = lax.dot_general(parts, perm[...], (((1,), (axis,)), ((), ())), preferred_element_type=F32)
+        rows = value.shape[0]
+        return (moved[:rows] + moved[rows : 2 * rows]) + moved[2 * rows :]
+
+    cell = lax.broadcasted_iota(jnp.int32, (2 * LANES, 2 * LANES), 0)
+    goal = lax.broadcasted_iota(jnp.int32, (2 * LANES, 2 * LANES), 1)
+    perm[...] = jnp.where(goal == (cell & 1) * LANES + (cell >> 1), 1.0, 0.0).astype(BF16)
+
     def pieces(body):
         def at(i, carry):
             row, layer = i // 2, lax.rem(i, 2)
-            for half in range(2):
-                body(row, layer, half, (layer, pl.ds(pl.multiple_of(row * BY, BY), BY), pl.ds(half * LANES, LANES)))
+            body(row, layer, (layer, pl.ds(pl.multiple_of(row * BY, BY), BY), slice(None)))
             return carry
 
         lax.fori_loop(0, 2 * NXB, at, 0)
 
-    def first_fields(row, layer, half, where):
-        c = cond[where]
-        sstage[COND, row, half, layer] = c
-        ids = (2 * space + layer) * (128 * 256) + row * (BY * 256) + half * LANES
-        ids = ids + lax.broadcasted_iota(jnp.int32, (BY, LANES), 0) * 256
-        ids = ids + lax.broadcasted_iota(jnp.int32, (BY, LANES), 1)
+    def first_fields(row, layer, where):
+        sources = [cond[where]]
         for t in range(2):
-            stage[U0, t, row, half, layer] = start[(t,) + where]
-            total = mem[(0, t) + where] + mem[(1, t) + where] + mem[(2, t) + where] + mem[(3, t) + where]
-            source = jnp.where(ids == src_cells[0, t], STRENGTH, 0.0) - jnp.where(ids == src_cells[1, t], STRENGTH, 0.0)
-            stage[R0, t, row, half, layer] = source + c * total
-
-    def later_fields(row, layer, half, where):
-        c, g = cond[where], chg[where]
-        rate = 1.0 / rlx[where]
+            sources.append(start[(t,) + where])
+            sources.append(mem[(0, t) + where] + mem[(1, t) + where] + mem[(2, t) + where] + mem[(3, t) + where])
+        moved = reorder(jnp.concatenate(sources, axis=0), 0)
+        for half in range(2):
+            c, u_a, q_a, u_b, q_b = (
+                moved[i * BY : (i + 1) * BY, half * LANES : (half + 1) * LANES] for i in range(5)
+            )
+            sstage[COND, row, half, layer] = c
+            ids = (2 * space + layer) * (128 * 256) + row * (BY * 256) + half
+            ids = ids + lax.broadcasted_iota(jnp.int32, (BY, LANES), 0) * 256
+            ids = ids + lax.broadcasted_iota(jnp.int32, (BY, LANES), 1) * 2
+            for t, (u, q) in enumerate(((u_a, q_a), (u_b, q_b))):
+                stage[U0, t, row, half, layer] = u
+                source = jnp.where(ids == src_cells[0, t], STRENGTH, 0.0)
+                source = source - jnp.where(ids == src_cells[1, t], STRENGTH, 0.0)
+                stage[R0, t, row, half, layer] = source + c * q
+
+    def later_fields(row, layer, where):
+        sources = [chg[where], rlx[where]] + [mem[(k, t) + where] for t in range(2) for k in range(4)]
+        moved = reorder(jnp.concatenate(sources, axis=0), 0)
+        for half in range(2):
+            later_half(
+                row, layer, half,
+                [moved[i * BY : (i + 1) * BY, half * LANES : (half + 1) * LANES] for i in range(10)],
+            )
+
+    def later_half(row, layer, half, values):
+        c, g = sstage[COND, row, half, layer], values[0]
+        rate = 1.0 / values[1]
         decays = [jnp.exp(-rate / ratio) for ratio in RATIOS]
         a0, a1, b0, b1 = (jnp.zeros((BY, LANES), F32) for _ in range(4))
         for k in range(4):
@@ -132,7 +164,7 @@
         for t in range(2):
             first, second, slope, slope_d = (jnp.zeros((BY, LANES), F32) for _ in range(4))
             for k in range(4):
-                scaled = decays[k] * mem[(k, t) + where]
+                scaled = decays[k] * values[2 + 4 * t + k]
                 first = first + scaled
                 second = second + decays[k] * scaled
                 tilt = scaled * (1.0 / RATIOS[k])
@@ -366,10 +398,8 @@
         c0 = ref[0, x, top : top + rows]
         c1 = ref[1, x, top : top + rows]
         lane = lax.broadcasted_iota(jnp.int32, (rows, LANES), 1)
-        next0, next1 = pltpu.roll(c0, LANES - 1, 1), pltpu.roll(c1, LANES - 1, 1)
-        last0, last1 = pltpu.roll(c0, 1, 1), pltpu.roll(c1, 1, 1)
-        z0 = jnp.where(lane == LANES - 1, next1, next0) + jnp.where(lane == 0, 0.0, last0)
-        z1 = jnp.where(lane == LANES - 1, 0.0, next1) + jnp.where(lane == 0, last0, last1)
+        z0 = c1 + jnp.where(lane == 0, 0.0, pltpu.roll(c1, 1, 1))
+        z1 = c0 + jnp.where(lane == LANES - 1, 0.0, pltpu.roll(c0, LANES - 1, 1))
         sums = []
         for half, z in ((0, z0), (1, z1)):
             total = ref[half, x + 1, top : top + rows] + ref[half, x - 1, top : top + rows]
@@ -394,13 +424,18 @@
             lax.fori_loop(s, EX - s, one, 0, unroll=UNROLL)
             source = goal
 
-    def locate(sign, k):
-        cells = dip[sign : sign + 1, pl.ds(pl.multiple_of(k * CHUNK, CHUNK), CHUNK)]
-        x, y, z = cells >> 15, (cells >> 8) & 127, cells & 255
-        own = ((x >> 4) == bx) & ((y >> 5) == gx)
-        row = jnp.where(own, (x & 15) * BY + (y & 31), -1)
-        hot = lax.broadcasted_iota(jnp.int32, (ROWS, CHUNK), 0) == row
-        return jnp.where(hot, 1.0, 0.0).astype(BF16), lax.broadcasted_iota(jnp.int32, (2 * LANES, CHUNK), 0) == z
+    def depth_of(sign, k):
+        z = dip[sign : sign + 1, pl.ds(pl.multiple_of(k * CHUNK, CHUNK), CHUNK)] & 255
+        return lax.broadcasted_iota(jnp.int32, (2 * LANES, CHUNK), 0) == (z & 1) * LANES + (z >> 1)
+
+    def mark_rows(k):
+        for sign in range(2):
+            cells = dip[sign : sign + 1, pl.ds(pl.multiple_of(k * CHUNK, CHUNK), CHUNK)]
+            x, y = cells >> 15, (cells >> 8) & 127
+            own = ((x >> 4) == bx) & ((y >> 5) == gx)
+            row = jnp.where(own, (x & 15) * BY + (y & 31), -1)
+            hot = lax.broadcasted_iota(jnp.int32, (ROWS, CHUNK), 0) == row
+            hots[sign, k] = jnp.where(hot, 1.0, 0.0).astype(BF16)
 
     def potential(n, half):
         if n == NSTEPS - 1:
@@ -417,10 +452,9 @@
         def at(k, carry):
             found = []
             for sign in range(2):
-                hot, depth = locate(sign, k)
-                both = jnp.dot(ut[...], hot, preferred_element_type=F32)
+                both = jnp.dot(ut[...], hots[sign, k], preferred_element_type=F32)
                 value = both[: 2 * LANES] + both[2 * LANES :]
-                found.append(jnp.sum(jnp.where(depth, value, 0.0), axis=0, keepdims=True))
+                found.append(jnp.sum(jnp.where(depth_of(sign, k), value, 0.0), axis=0, keepdims=True))
             part[n, :, pl.ds(pl.multiple_of(k * CHUNK, CHUNK), CHUNK)] = found[0] - found[1]
             return carry
 
@@ -432,12 +466,11 @@
         def at(k, carry):
             value = res[n, :, pl.ds(pl.multiple_of(k * CHUNK, CHUNK), CHUNK)]
             for sign in range(2):
-                hot, depth = locate(sign, k)
-                placed = jnp.where(depth, value if sign == 0 else -value, 0.0)
+                placed = jnp.where(depth_of(sign, k), value if sign == 0 else -value, 0.0)
                 high = placed.astype(BF16)
                 low = (placed - high.astype(F32)).astype(BF16)
                 acc[n - 1] += lax.dot_general(
-                    hot, jnp.concatenate([high, low], axis=0), (((1,), (1,)), ((), ())), preferred_element_type=F32
+                    hots[sign, k], jnp.concatenate([high, low], axis=0), (((1,), (1,)), ((), ())), preferred_element_type=F32
                 )
             return carry
 
@@ -450,10 +483,45 @@
             + acc[n - 1, rows, (2 + half) * LANES : (3 + half) * LANES]
         )
 
+    def row_copy(n, p):
+        to = lax.rem(gx + p, NXB)
+        return remote(
+            part.at[n], prx.at[gx, n], psend.at[0, n, to], precv.at[0, n, gx], {"space": device(bx, to, mine)}
+        )
+
+    def row_wait(n, p):
+        of = lax.rem(gx + p, NXB)
+        here = prx.at[of, n]
+        remote(here, here, psend.at[0, n, of], precv.at[0, n, of], {"space": device(bx, of, mine)}).wait_recv()
+
+    def row_copies(n):
+        over(4, lambda p: row_copy(n, p).start(), 1)
+        prx[gx, n] = part[n]
+
+    def row_sums(n):
+        over(4, functools.partial(row_wait, n), 1)
+        res[n] = (prx[0, n] + prx[1, n]) + (prx[2, n] + prx[3, n])
+
+    def col_copy(n, p):
+        to = lax.rem(bx + p, NB)
+        return remote(
+            res.at[n], pry.at[bx, n], psend.at[1, n, to], precv.at[1, n, bx], {"space": device(to, gx, mine)}
+        )
+
+    def col_wait(n, p):
+        of = lax.rem(bx + p, NB)
+        here = pry.at[of, n]
+        remote(here, here, psend.at[1, n, of], precv.at[1, n, of], {"space": device(of, gx, mine)}).wait_recv()
+
+    def col_copies(n):
+        over(4, lambda p: col_copy(n, p).start(), 1)
+        pry[bx, n] = res[n]
+
     spread_static(COND)
     for load in loads[3:]:
         load.wait()
     pieces(later_fields)
+    over(NDIP // CHUNK, mark_rows)
     take_field(U0)
     halo_start(entry.at[0], VTOP, 0)
     take_static(COND)
@@ -467,13 +535,12 @@
     take_field(R0)
     halo_start(rhs.at[0], HALO, 5)
     send_static(F1)
-    send_static(F2)
     halo_wait(entry.at[0], VTOP, 0)
     halo_wait(inv, HALO, 8)
     halo_wait(rhs.at[0], HALO, 5)
     send_field(R1)
+    send_static(F2)
     spread_static(F1)
-    spread_static(F2)
 
     def block_of(k, half, x):
         return entry[k, half, HALO + x, VTOP : VTOP + BY]
@@ -505,10 +572,12 @@
 
     over_x(step_one)
     halo_start(rhs.at[1], HALO, 6)
+    spread_static(F2)
     obs_pair_in.wait_recv()
     over(SLOTS, lambda p: obs_copy(p, 0).start(), 1)
     over(SLOTS, lambda p: obs_copy(p, 1).start(), 1)
     gather(0)
+    row_copies(0)
     halo_wait(entry.at[1], VTOP, 1)
     halo_wait(rhs.at[1], HALO, 6)
     send_field(R2)
@@ -531,6 +600,9 @@
     over(SLOTS, lambda p: obs_wait(p, 1), 1)
     obs_rows(True).start()
     gather(1)
+    row_copies(1)
+    row_sums(0)
+    col_copies(0)
     halo_wait(entry.at[2], VTOP, 2)
     halo_wait(rhs.at[2], HALO, 7)
     forward(2)
@@ -569,31 +641,14 @@
     gather(2)
     obs_rows(False).wait_recv()
 
-    def row_copy(p):
-        to = lax.rem(gx + p, NXB)
-        return remote(part, prx.at[gx], psend.at[0, to], precv.at[0, gx], {"space": device(bx, to, mine)})
-
-    def row_wait(p):
-        of = lax.rem(gx + p, NXB)
-        remote(part, prx.at[of], psend.at[0, of], precv.at[0, of], {"space": device(bx, of, mine)}).wait_recv()
-
-    over(4, lambda p: row_copy(p).start(), 1)
-    prx[gx] = part[...]
-    over(4, row_wait, 1)
-    res[...] = (prx[0] + prx[1]) + (prx[2] + prx[3])
-
-    def col_copy(p):
-        to = lax.rem(bx + p, NB)
-        return remote(res, pry.at[bx], psend.at[1, to], precv.at[1, bx], {"space": device(to, gx, mine)})
-
-    def col_wait(p):
-        of = lax.rem(bx + p, NB)
-        remote(res, pry.at[of], psend.at[1, of], precv.at[1, of], {"space": device(of, gx, mine)}).wait_recv()
-
-    over(4, lambda p: col_copy(p).start(), 1)
-    pry[bx] = res[...]
-    over(4, col_wait, 1)
-    over(4, lambda p: col_copy(p).wait_send(), 1)
+    row_copies(2)
+    row_sums(1)
+    col_copies(1)
+    row_sums(2)
+    col_copies(2)
+    for n in range(NSTEPS):
+        over(4, functools.partial(col_wait, n), 1)
+        over(4, lambda p: col_copy(n, p).wait_send(), 1)
     squares = jnp.zeros((1, NDIP), F32)
     for n in range(NSTEPS):
         volts = live[...] * ((pry[0, n] + pry[1, n]) + (pry[2, n] + pry[3, n]))
@@ -713,9 +768,9 @@
     over(NXB, gradients)
     for f, out in ((0, gc_out), (1, gt_out)):
         over(4, functools.partial(tx_wait, f), 1)
-        for half in range(2):
-            value = (rz[f, 0, half] + rz[f, 1, half]) + (rz[f, 2, half] + rz[f, 3, half])
-            out[:, :, half * LANES : (half + 1) * LANES] = value * scale.reshape(1, 1, 1)
+        halves = [(rz[f, 0, half] + rz[f, 1, half]) + (rz[f, 2, half] + rz[f, 3, half]) for half in range(2)]
+        value = reorder(jnp.concatenate([half.reshape(2 * BY, LANES) for half in halves], axis=1), 1)
+        out[...] = value.reshape(2, BY, 2 * LANES) * scale.reshape(1, 1, 1)
 
     for f in range(4):
         finish(f, field_copy)
@@ -726,7 +781,8 @@
     for which in range(2):
         over(SLOTS, lambda p: obs_copy(p, which).wait_send(), 1)
     obs_rows(True).wait_send()
-    over(4, lambda p: row_copy(p).wait_send(), 1)
+    for n in range(NSTEPS):
+        over(4, lambda p: row_copy(n, p).wait_send(), 1)
     over(4, lambda p: sq_copy(p).wait_send(), 1)
     for f in range(4):
         finish(f, back_copy)
@@ -746,6 +802,8 @@
         slab, slab, slab,
         pltpu.VMEM((2, 2, 128, 2 * LANES), F32),
         pltpu.VMEM((4, 2, 2, 128, 2 * LANES), F32),
+        pltpu.VMEM((2 * LANES, 2 * LANES), BF16),
+        pltpu.VMEM((2, NDIP // CHUNK, ROWS, CHUNK), BF16),
         pltpu.VMEM((4, 2, NXB, 2, 2, BY, LANES), F32),
         pltpu.VMEM((3, NXB, 2, 2, BY, LANES), F32),
         pltpu.VMEM((2, 2, NXB, 2, 2, BY, LANES), F32),
@@ -779,7 +837,7 @@
         dma((3, 4)), dma((3, 4)),
         dma((9, 8)), dma((9, 8)),
         dma((2, SLOTS)), dma((2, SLOTS)),
-        dma((2, 4)), dma((2, 4)),
+        dma((2, NSTEPS, 4)), dma((2, NSTEPS, 4)),
         dma((4,)), dma((4,)),
         dma((4, SLOTS)), dma((4, SLOTS)),
         dma((3, 4)), dma((3, 4)),

time: 176 us -> 164 us (0.932)
  Pallas kernels: 169 us -> 157 us
    pallas_call x1, Pallas kernels: 169 us -> 157 us  [on_device(): pl.pallas_call(kernel, out_shape=(jax.ShapeDtypeStruct((NSTEPS, 2, LANES)...]
where the time goes in v4:
time: 164 us; the launch traced here: 163 us
  Pallas kernels  157 us (96%)
  local copies, waits for them, and re-layouts  4.21 us (3%)
  between operations  2.4 us (1%)
    pallas_call x1, Pallas kernels, on_device(): pl.pallas_call(kernel, out_shape=(jax.ShapeDtypeStruct((NSTEPS, 2, LANES)...  157 us
    unnamed x3, local copies, waits for them, and re-layouts  4.21 us

profile of v4, /device:TPU:19, one launch (start us, length us, event | category | flops | bytes accessed | tf_op | source)
XLA Modules:
  0.0 163.3 jit_solution(7956313296332574720)
XLA Ops:
  0.6 156.7 %shard_map.120 = (f32[3,2,128]{2,1,0:T(2,128)}, f32[1,1]{1,0:T(1,128)}, f32[2,32,256]{2,1,0:T(8,128)}, f32[2,32,256]{2,1,0:T(8,128)}) custom-call(f32[2,128,256]{2,1,0:T(8,128)} %cond_hbm.1, f32[2,128,256]{2,1,0:T(8,128)} %chg_hbm.1, f32[2,128,256]{2,1,0:T(8,128)} %rlx_hbm.1, f32[2,2,128,256]{3,2,1,0:T(8,128)} %start_hbm.1, f32[4,2,2,128,256]{4,3,2,1,0:T(8,128)} %mem_hbm.1, ...), custom_call_target="tpu_custom_call" | custom-call | tf_op jit(solution)/shard_map/pallas_call | solution.py:845
  157.4 1.3 copy.17
  159.3 1.5 copy.19
  160.7 1.5 copy.20

commit v5 on v4

--- a/solution.py
+++ b/solution.py
@@ -25,6 +25,8 @@
 VTOP = PAD + HALO
 NDIP = 4096
 CHUNK = 512
+HALF = NDIP // 2
+HALF_CHUNKS = HALF // CHUNK
 ROWS = BX * BY
 UNROLL = 8
 U0, R0, R1, R2 = range(4)
@@ -47,7 +49,7 @@
     cond, chg, rlx, start, mem,
     perm, hots, stage, sstage, tilts, factors, blk, sblk, entry, va, vb,
     inv, rhs, ulast, adj, back,
-    ut, acc, part, prx, pry, res, obs_all, live, vswap, sq, sqc, sqz,
+    ut, acc, part, prx, pry, rows, volts, res, obs_all, live, vswap, sq, sqc, sqz,
     rx, rsum, rz,
     lsem, fsend, frecv, ssend, srecv, zsend, zrecv, hsend, hrecv, osend, orecv, psend, precv, qsend, qrecv,
     gsend, grecv, tsend, trecv,
@@ -442,13 +444,14 @@
             return ulast[half]
         return entry[n + 1, half, HALO : HALO + BX, VTOP : VTOP + BY]
 
-    def gather(n):
+    def gather_table(n):
         for half in range(2):
             rows = potential(n, half).reshape(ROWS, LANES).T
             high = rows.astype(BF16)
             ut[half * LANES : (half + 1) * LANES, :] = high
             ut[(2 + half) * LANES : (3 + half) * LANES, :] = (rows - high.astype(F32)).astype(BF16)
 
+    def gather_part(n, h):
         def at(k, carry):
             found = []
             for sign in range(2):
@@ -458,10 +461,16 @@
             part[n, :, pl.ds(pl.multiple_of(k * CHUNK, CHUNK), CHUNK)] = found[0] - found[1]
             return carry
 
-        lax.fori_loop(0, NDIP // CHUNK, at, 0)
-
-    def scatter(n):
-        acc[n - 1] = jnp.zeros((ROWS, 4 * LANES), F32)
+        lax.fori_loop(h * HALF_CHUNKS, (h + 1) * HALF_CHUNKS, at, 0)
+
+    def gather(n):
+        gather_table(n)
+        for h in range(2):
+            gather_part(n, h)
+
+    def scatter(n, h):
+        if h == 0:
+            acc[n - 1] = jnp.zeros((ROWS, 4 * LANES), F32)
 
         def at(k, carry):
             value = res[n, :, pl.ds(pl.multiple_of(k * CHUNK, CHUNK), CHUNK)]
@@ -474,7 +483,7 @@
                 )
             return carry
 
-        lax.fori_loop(0, NDIP // CHUNK, at, 0)
+        lax.fori_loop(h * HALF_CHUNKS, (h + 1) * HALF_CHUNKS, at, 0)
 
     def injected(n, half, x):
         rows = pl.ds(pl.multiple_of(x * BY, BY), BY)
@@ -483,39 +492,84 @@
             + acc[n - 1, rows, (2 + half) * LANES : (3 + half) * LANES]
         )
 
-    def row_copy(n, p):
+    def span(h):
+        return pl.ds(h * HALF, HALF)
+
+    def row_copy(n, h, p):
         to = lax.rem(gx + p, NXB)
         return remote(
-            part.at[n], prx.at[gx, n], psend.at[0, n, to], precv.at[0, n, gx], {"space": device(bx, to, mine)}
+            part.at[n, :, span(h)], prx.at[gx, n, :, span(h)], psend.at[0, n, h, to], precv.at[0, n, h, gx],
+            {"space": device(bx, to, mine)},
         )
 
-    def row_wait(n, p):
+    def row_wait(n, h, p):
         of = lax.rem(gx + p, NXB)
-        here = prx.at[of, n]
-        remote(here, here, psend.at[0, n, of], precv.at[0, n, of], {"space": device(bx, of, mine)}).wait_recv()
-
-    def row_copies(n):
-        over(4, lambda p: row_copy(n, p).start(), 1)
-        prx[gx, n] = part[n]
-
-    def row_sums(n):
-        over(4, functools.partial(row_wait, n), 1)
-        res[n] = (prx[0, n] + prx[1, n]) + (prx[2, n] + prx[3, n])
-
-    def col_copy(n, p):
+        here = prx.at[of, n, :, span(h)]
+        remote(
+            here, here, psend.at[0, n, h, of], precv.at[0, n, h, of], {"space": device(bx, of, mine)}
+        ).wait_recv()
+
+    def row_copies(n, h):
+        over(4, lambda p: row_copy(n, h, p).start(), 1)
+        prx[gx, n, :, span(h)] = part[n, :, span(h)]
+
+    def col_copy(n, h, p):
         to = lax.rem(bx + p, NB)
         return remote(
-            res.at[n], pry.at[bx, n], psend.at[1, n, to], precv.at[1, n, bx], {"space": device(to, gx, mine)}
+            rows.at[n, :, span(h)], pry.at[bx, n, :, span(h)], psend.at[1, n, h, to], precv.at[1, n, h, bx],
+            {"space": device(to, gx, mine)},
         )
 
-    def col_wait(n, p):
+    def col_wait(n, h, p):
         of = lax.rem(bx + p, NB)
-        here = pry.at[of, n]
-        remote(here, here, psend.at[1, n, of], precv.at[1, n, of], {"space": device(of, gx, mine)}).wait_recv()
-
-    def col_copies(n):
-        over(4, lambda p: col_copy(n, p).start(), 1)
-        pry[bx, n] = res[n]
+        here = pry.at[of, n, :, span(h)]
+        remote(
+            here, here, psend.at[1, n, h, of], precv.at[1, n, h, of], {"space": device(of, gx, mine)}
+        ).wait_recv()
+
+    def row_sums(n, h):
+        over(4, functools.partial(row_wait, n, h), 1)
+        at = (n, slice(None), span(h))
+        rows[at] = (prx[(0,) + at] + prx[(1,) + at]) + (prx[(2,) + at] + prx[(3,) + at])
+        over(4, lambda p: col_copy(n, h, p).start(), 1)
+        pry[(bx,) + at] = rows[at]
+
+    def residual(n, h):
+        over(4, functools.partial(col_wait, n, h), 1)
+        at = (n, slice(None), span(h))
+        alive = live[:, span(h)]
+        value = alive * ((pry[(0,) + at] + pry[(1,) + at]) + (pry[(2,) + at] + pry[(3,) + at]))
+        volts[at] = value
+        res[at] = alive * (value - obs_all[at])
+
+    def back_copy(f, p):
+        j = lax.rem(p + slot, SLOTS)
+        layers = pl.ds(HALO + 2 * j, 2)
+        if f in (POT0, POT1):
+            here = entry.at[f + 1, :, layers, pl.ds(VTOP, BY)]
+        else:
+            here = adj.at[DUAL1 - f, :, layers, pl.ds(HALO, BY)]
+        to = bx * SLOTS + j
+        return to, remote(here, rx.at[f, gx, mine], gsend.at[f, j], grecv.at[f, 2 * gx + mine], {"space": to})
+
+    def send_back(f):
+        begin(f, back_copy)
+
+        def keep():
+            layers = pl.ds(HALO + 2 * slot, 2)
+            if f in (POT0, POT1):
+                rx[f, gx, mine] = entry[f + 1, :, layers, VTOP : VTOP + BY]
+            else:
+                rx[f, gx, mine] = adj[DUAL1 - f, :, layers, HALO : HALO + BY]
+
+        pl.when(bx == yp)(keep)
+
+    def back_wait(f, q):
+        x, t = q // 2, lax.rem(q, 2)
+        of = device(yp, x, t)
+        here = rx.at[f, x, t]
+        copy = remote(here, here, gsend.at[f, q], grecv.at[f, q], {"space": of})
+        pl.when(of != space)(copy.wait_recv)
 
     spread_static(COND)
     for load in loads[3:]:
@@ -577,7 +631,8 @@
     over(SLOTS, lambda p: obs_copy(p, 0).start(), 1)
     over(SLOTS, lambda p: obs_copy(p, 1).start(), 1)
     gather(0)
-    row_copies(0)
+    for h in range(2):
+        row_copies(0, h)
     halo_wait(entry.at[1], VTOP, 1)
     halo_wait(rhs.at[1], HALO, 6)
     send_field(R2)
@@ -600,90 +655,24 @@
     over(SLOTS, lambda p: obs_wait(p, 1), 1)
     obs_rows(True).start()
     gather(1)
-    row_copies(1)
-    row_sums(0)
-    col_copies(0)
+    for h in range(2):
+        row_copies(1, h)
+        row_sums(0, h)
     halo_wait(entry.at[2], VTOP, 2)
     halo_wait(rhs.at[2], HALO, 7)
+    send_back(POT0)
     forward(2)
 
-    def back_copy(f, p):
-        j = lax.rem(p + slot, SLOTS)
-        layers = pl.ds(HALO + 2 * j, 2)
-        if f in (POT0, POT1):
-            here = entry.at[f + 1, :, layers, pl.ds(VTOP, BY)]
-        else:
-            here = adj.at[DUAL1 - f, :, layers, pl.ds(HALO, BY)]
-        to = bx * SLOTS + j
-        return to, remote(here, rx.at[f, gx, mine], gsend.at[f, j], grecv.at[f, 2 * gx + mine], {"space": to})
-
-    def send_back(f):
-        begin(f, back_copy)
-
-        def keep():
-            layers = pl.ds(HALO + 2 * slot, 2)
-            if f in (POT0, POT1):
-                rx[f, gx, mine] = entry[f + 1, :, layers, VTOP : VTOP + BY]
-            else:
-                rx[f, gx, mine] = adj[DUAL1 - f, :, layers, HALO : HALO + BY]
-
-        pl.when(bx == yp)(keep)
-
-    def back_wait(f, q):
-        x, t = q // 2, lax.rem(q, 2)
-        of = device(yp, x, t)
-        here = rx.at[f, x, t]
-        copy = remote(here, here, gsend.at[f, q], grecv.at[f, q], {"space": of})
-        pl.when(of != space)(copy.wait_recv)
-
-    send_back(POT0)
-    send_back(POT1)
-    gather(2)
+    gather_table(2)
+    gather_part(2, 0)
+    row_copies(2, 0)
+    gather_part(2, 1)
+    row_copies(2, 1)
     obs_rows(False).wait_recv()
-
-    row_copies(2)
-    row_sums(1)
-    col_copies(1)
-    row_sums(2)
-    col_copies(2)
-    for n in range(NSTEPS):
-        over(4, functools.partial(col_wait, n), 1)
-        over(4, lambda p: col_copy(n, p).wait_send(), 1)
-    squares = jnp.zeros((1, NDIP), F32)
-    for n in range(NSTEPS):
-        volts = live[...] * ((pry[0, n] + pry[1, n]) + (pry[2, n] + pry[3, n]))
-        part_resid = live[...] * (volts - obs_all[n])
-        pry[0, n] = volts
-        res[n] = part_resid
-        squares = squares + part_resid * part_resid
-
-    own = pl.ds(pl.multiple_of(space * LANES, LANES), LANES)
-    other = pl.ds(pl.multiple_of(partner * LANES, LANES), LANES)
-    swap = remote(pry.at[0, :, :, other], vswap.at[pl.ds(6, 3)], qsend.at[2], qrecv.at[2], {"space": partner})
-    swap.start()
-    lanes = squares[:, 0:LANES]
-    for j in range(1, NDIP // LANES):
-        lanes = lanes + squares[:, j * LANES : (j + 1) * LANES]
-    sq[...] = lanes
-    pair = remote(sq, sqc, qsend.at[3], qrecv.at[3], {"space": partner})
-    pair.start()
-    for n in range(NSTEPS):
-        volts_out[n, pl.ds(mine, 1), :] = pry[0, n, :, own]
-    swap.wait()
-    for n in range(NSTEPS):
-        volts_out[n, pl.ds(1 - mine, 1), :] = vswap[6 + n]
-    pair.wait()
-    sqz[tx] = sq[...] + sqc[...]
-
-    def sq_copy(p):
-        to = lax.rem(tx + p, 4)
-        return remote(sqz.at[tx], sqz.at[tx], tsend.at[2, to], trecv.at[2, tx], {"tx": to})
-
-    def sq_wait(p):
-        of = lax.rem(tx + p, 4)
-        remote(sqz.at[of], sqz.at[of], tsend.at[2, of], trecv.at[2, of], {"tx": of}).wait_recv()
-
-    over(4, lambda p: sq_copy(p).start(), 1)
+    row_sums(2, 0)
+    row_sums(2, 1)
+    for h in range(2):
+        row_sums(1, h)
 
     def begin_adjoint(n):
         def body(x):
@@ -709,11 +698,50 @@
 
         sweeps(entry.at[5 - n], JACOBI if n == 2 else JACOBI - 1, body, closing)
 
-    scatter(2)
+    for h in range(2):
+        residual(2, h)
+        scatter(2, h)
     begin_adjoint(2)
     halo_start(entry.at[3], VTOP, 3)
-    scatter(1)
+    for h in range(2):
+        residual(1, h)
+        scatter(1, h)
+        residual(0, h)
+
+    squares = jnp.zeros((1, NDIP), F32)
+    for n in range(NSTEPS):
+        squares = squares + res[n] * res[n]
+
+    own = pl.ds(pl.multiple_of(space * LANES, LANES), LANES)
+    other = pl.ds(pl.multiple_of(partner * LANES, LANES), LANES)
+    swap = remote(volts.at[:, :, other], vswap.at[pl.ds(6, 3)], qsend.at[2], qrecv.at[2], {"space": partner})
+    swap.start()
+    lanes = squares[:, 0:LANES]
+    for j in range(1, NDIP // LANES):
+        lanes = lanes + squares[:, j * LANES : (j + 1) * LANES]
+    sq[...] = lanes
+    pair = remote(sq, sqc, qsend.at[3], qrecv.at[3], {"space": partner})
+    pair.start()
+    for n in range(NSTEPS):
+        volts_out[n, pl.ds(mine, 1), :] = volts[n, :, own]
+    swap.wait()
+    for n in range(NSTEPS):
+        volts_out[n, pl.ds(1 - mine, 1), :] = vswap[6 + n]
+    pair.wait()
+    sqz[tx] = sq[...] + sqc[...]
+
+    def sq_copy(p):
+        to = lax.rem(tx + p, 4)
+        return remote(sqz.at[tx], sqz.at[tx], tsend.at[2, to], trecv.at[2, tx], {"tx": to})
+
+    def sq_wait(p):
+        of = lax.rem(tx + p, 4)
+        remote(sqz.at[of], sqz.at[of], tsend.at[2, of], trecv.at[2, of], {"tx": of}).wait_recv()
+
+    over(4, lambda p: sq_copy(p).start(), 1)
+
     halo_wait(entry.at[3], VTOP, 3)
+    send_back(POT1)
     adjoint(2)
     begin_adjoint(1)
     halo_start(entry.at[4], VTOP, 4)
@@ -782,12 +810,23 @@
         over(SLOTS, lambda p: obs_copy(p, which).wait_send(), 1)
     obs_rows(True).wait_send()
     for n in range(NSTEPS):
-        over(4, lambda p: row_copy(n, p).wait_send(), 1)
+        for h in range(2):
+            over(4, lambda p: row_copy(n, h, p).wait_send(), 1)
+            over(4, lambda p: col_copy(n, h, p).wait_send(), 1)
     over(4, lambda p: sq_copy(p).wait_send(), 1)
     for f in range(4):
         finish(f, back_copy)
     for f in range(2):
         over(4, lambda p: tx_copy(f, lax.rem(tx + p, 4)).wait_send(), 1)
+
+
+def hand_over(*refs):
+    given, made, sems = refs[:4], refs[4:8], refs[8]
+    copies = [pltpu.make_async_copy(a, b, sems.at[i]) for i, (a, b) in enumerate(zip(given, made))]
+    for copy in copies:
+        copy.start()
+    for copy in copies:
+        copy.wait()
 
 
 def on_device(cond, chg, rlx, start, mem, src_cells, dip, counts, obs):
@@ -824,6 +863,8 @@
         pltpu.VMEM((NB, NSTEPS, 1, NDIP), F32),
         pltpu.VMEM((NSTEPS, 1, NDIP), F32),
         pltpu.VMEM((NSTEPS, 1, NDIP), F32),
+        pltpu.VMEM((NSTEPS, 1, NDIP), F32),
+        pltpu.VMEM((NSTEPS, 1, NDIP), F32),
         pltpu.VMEM((1, NDIP), F32),
         pltpu.VMEM((9, 1, LANES), F32),
         pltpu.VMEM((1, LANES), F32),
@@ -837,7 +878,7 @@
         dma((3, 4)), dma((3, 4)),
         dma((9, 8)), dma((9, 8)),
         dma((2, SLOTS)), dma((2, SLOTS)),
-        dma((2, NSTEPS, 4)), dma((2, NSTEPS, 4)),
+        dma((2, NSTEPS, 2, 4)), dma((2, NSTEPS, 2, 4)),
         dma((4,)), dma((4,)),
         dma((4, SLOTS)), dma((4, SLOTS)),
         dma((3, 4)), dma((3, 4)),
@@ -855,6 +896,14 @@
         scratch_shapes=scratch,
         compiler_params=pltpu.CompilerParams(has_side_effects=True, collective_id=0, vmem_limit_bytes=60 << 20),
     )(cond, chg, rlx, start, mem, src_cells, dip, counts, obs)
+    results = (volts, misfit, grad_c, grad_t)
+    volts, misfit, grad_c, grad_t = pl.pallas_call(
+        hand_over,
+        out_shape=tuple(jax.ShapeDtypeStruct(a.shape, F32) for a in results),
+        in_specs=[whole] * 4,
+        out_specs=(whole,) * 4,
+        scratch_shapes=[dma((4,))],
+    )(*results)
     return (volts, misfit.reshape(()), grad_c, grad_t)
 
 

time: 164 us -> 158 us (0.963)
  local copies, waits for them, and re-layouts: 4.21 us -> 0 us
    pallas_call x1, Pallas kernels: 157 us -> 150 us  [on_device(): pl.pallas_call(kernel, out_shape=(jax.ShapeDtypeStruct((NSTEPS, 2, LANES)...]
    pallas_call x0 -> x1, Pallas kernels: none -> 5.83 us  [on_device(): pl.pallas_call(hand_over, out_shape=tuple((jax.ShapeDtypeStruct(a.shape,...]
    unnamed x3 -> x0, local copies, waits for them, and re-layouts: 4.21 us -> none
where the time goes in v5:
time: 158 us; the launch traced here: 157 us
  Pallas kernels  156 us (99%)
    pallas_call x1, Pallas kernels, on_device(): pl.pallas_call(kernel, out_shape=(jax.ShapeDtypeStruct((NSTEPS, 2, LANES)...  150 us
    pallas_call x1, Pallas kernels, on_device(): pl.pallas_call(hand_over, out_shape=tuple((jax.ShapeDtypeStruct(a.shape,...  5.83 us

profile of v5, /device:TPU:19, one launch (start us, length us, event | category | flops | bytes accessed | tf_op | source)
XLA Modules:
  0.0 157.0 jit_solution(14891467977872989234)
XLA Ops:
  0.6 150.4 %shard_map.120 = (f32[3,2,128]{2,1,0:T(2,128)}, f32[1,1]{1,0:T(1,128)}, f32[2,32,256]{2,1,0:T(8,128)}, f32[2,32,256]{2,1,0:T(8,128)}) custom-call(f32[2,128,256]{2,1,0:T(8,128)} %cond_hbm.1, f32[2,128,256]{2,1,0:T(8,128)} %chg_hbm.1, f32[2,128,256]{2,1,0:T(8,128)} %rlx_hbm.1, f32[2,2,128,256]{3,2,1,0:T(8,128)} %start_hbm.1, f32[4,2,2,128,256]{4,3,2,1,0:T(8,128)} %mem_hbm.1, ...), custom_call_target="tpu_custom_call" | custom-call | tf_op jit(solution)/shard_map/pallas_call | solution.py:886
  151.0 5.8 %shard_map.121 = (f32[3,2,128]{2,1,0:T(2,128)}, f32[1,1]{1,0:T(1,128)}, f32[2,32,256]{2,1,0:T(8,128)}, f32[2,32,256]{2,1,0:T(8,128)}) custom-call(f32[3,2,128]{2,1,0:T(2,128)} %get-tuple-element.12.refs_0_, f32[1,1]{1,0:T(1,128)} %get-tuple-element.13.refs_1_, f32[2,32,256]{2,1,0:T(8,128)} %get-tuple-element.14.refs_2_, f32[2,32,256]{2,1,0:T(8,128)} %get-tuple-element.15.refs_3_), custom_call_target="tpu_custom_call" | custom-call | tf_op jit(solution)/shard_map/pallas_call | solution.py:900

commit v6 on v5

--- a/solution.py
+++ b/solution.py
@@ -34,7 +34,7 @@
 KA0, KA1, KB0, KB1 = range(4)
 POT0, POT1, DUAL2, DUAL1 = range(4)
 SPACES = 32
-SIDES = tuple((i, j) for i in (-1, 0, 1) for j in (-1, 0, 1) if (i, j) != (0, 0))
+SIDES = ((0, -1), (0, 1), (-1, 0), (1, 0), (-1, -1), (-1, 1), (1, -1), (1, 1))
 
 
 def remote(src, dst, send, recv, device):
@@ -365,7 +365,8 @@
 
     def halo(ref, top, which):
         width = HALO if top == VTOP else HALO - 1
-        copies = []
+        copies, passed = [], []
+        even = lax.rem(bx, 2) == 0
         for side, (i, j) in enumerate(SIDES):
             deep = width if j == 0 else width - 1
             layers = {-1: (HALO, deep, HALO + BX), 1: (HALO + BX - deep, deep, HALO - deep), 0: (HALO, BX, HALO)}[i]
@@ -373,21 +374,40 @@
             sends = (bx + i >= 0) & (bx + i < NB) & (gx + j >= 0) & (gx + j < NXB)
             takes = (bx - i >= 0) & (bx - i < NB) & (gx - j >= 0) & (gx - j < NXB)
             to = device(lax.rem(bx + i + NB, NB), lax.rem(gx + j + NXB, NXB), mine)
-            copies.append((sends, takes, remote(
+            if i != 0 and j != 0:
+                joint = even if i == 1 else jnp.logical_not(even)
+                sends = sends & jnp.logical_not(joint)
+                gives = joint & (gx - j >= 0) & (gx - j < NXB)
+                passed.append((gives, remote(
+                    ref.at[:, pl.ds(layers[0], layers[1]), pl.ds(rows[2], rows[1])],
+                    ref.at[:, pl.ds(layers[2], layers[1]), pl.ds(rows[2], rows[1])],
+                    hsend.at[which, side], hrecv.at[which, side],
+                    {"space": device(lax.rem(bx + i + NB, NB), gx, mine)},
+                )))
+            copies.append((i == 0, sends, takes, remote(
                 ref.at[:, pl.ds(layers[0], layers[1]), pl.ds(rows[0], rows[1])],
                 ref.at[:, pl.ds(layers[2], layers[1]), pl.ds(rows[2], rows[1])],
                 hsend.at[which, side], hrecv.at[which, side], {"space": to},
             )))
-        return copies
+        return copies, passed
 
     def halo_start(ref, top, which):
-        for sends, _, copy in halo(ref, top, which):
+        for _, sends, _, copy in halo(ref, top, which)[0]:
             pl.when(sends)(copy.start)
 
     def halo_wait(ref, top, which):
-        for sends, takes, copy in halo(ref, top, which):
-            pl.when(takes)(copy.wait_recv)
+        copies, passed = halo(ref, top, which)
+        for along_rows, _, takes, copy in copies:
+            if along_rows:
+                pl.when(takes)(copy.wait_recv)
+        for gives, copy in passed:
+            pl.when(gives)(copy.start)
+        for along_rows, sends, takes, copy in copies:
+            if not along_rows:
+                pl.when(takes)(copy.wait_recv)
             pl.when(sends)(copy.wait_send)
+        for gives, copy in passed:
+            pl.when(gives)(copy.wait_send)
 
     def over_x(body, unroll=1):
         def at(x, carry):

time: 158 us -> 155 us (0.981)
  Pallas kernels: 156 us -> 154 us
    pallas_call x1, Pallas kernels: 150 us -> 148 us  [on_device(): pl.pallas_call(kernel, out_shape=(jax.ShapeDtypeStruct((NSTEPS, 2, LANES)...]
where the time goes in v6:
time: 155 us; the launch traced here: 154 us
  Pallas kernels  154 us (99%)
    pallas_call x1, Pallas kernels, on_device(): pl.pallas_call(kernel, out_shape=(jax.ShapeDtypeStruct((NSTEPS, 2, LANES)...  148 us
    pallas_call x1, Pallas kernels, on_device(): pl.pallas_call(hand_over, out_shape=tuple((jax.ShapeDtypeStruct(a.shape,...  5.83 us

profile of v6, /device:TPU:19, one launch (start us, length us, event | category | flops | bytes accessed | tf_op | source)
XLA Modules:
  0.0 154.5 jit_solution(8830566223302822157)
XLA Ops:
  0.6 147.8 %shard_map.120 = (f32[3,2,128]{2,1,0:T(2,128)}, f32[1,1]{1,0:T(1,128)}, f32[2,32,256]{2,1,0:T(8,128)}, f32[2,32,256]{2,1,0:T(8,128)}) custom-call(f32[2,128,256]{2,1,0:T(8,128)} %cond_hbm.1, f32[2,128,256]{2,1,0:T(8,128)} %chg_hbm.1, f32[2,128,256]{2,1,0:T(8,128)} %rlx_hbm.1, f32[2,2,128,256]{3,2,1,0:T(8,128)} %start_hbm.1, f32[4,2,2,128,256]{4,3,2,1,0:T(8,128)} %mem_hbm.1, ...), custom_call_target="tpu_custom_call" | custom-call | tf_op jit(solution)/shard_map/pallas_call | solution.py:906
  148.5 5.8 %shard_map.121 = (f32[3,2,128]{2,1,0:T(2,128)}, f32[1,1]{1,0:T(1,128)}, f32[2,32,256]{2,1,0:T(8,128)}, f32[2,32,256]{2,1,0:T(8,128)}) custom-call(f32[3,2,128]{2,1,0:T(2,128)} %get-tuple-element.12.refs_0_, f32[1,1]{1,0:T(1,128)} %get-tuple-element.13.refs_1_, f32[2,32,256]{2,1,0:T(8,128)} %get-tuple-element.14.refs_2_, f32[2,32,256]{2,1,0:T(8,128)} %get-tuple-element.15.refs_3_), custom_call_target="tpu_custom_call" | custom-call | tf_op jit(solution)/shard_map/pallas_call | solution.py:920
